TPU v7x, 32 devices: a whole 2x2x4 slice. The times are simulated.
32 devices in a mesh: section: 2 (over y), expert: 4 (over z), hid: 4 (over x, core).
Axes of the slice: x: 2, y: 2, z: 4, core: 2. Of those that a mesh axis runs over, the one named last changes fastest.
Arguments:
- saved_input: bfloat16 [2, 512, 4096], P('section', 'expert', 'hid'), may hold values from -6 to 6
- cotangent: bfloat16 [2, 512, 4096], P('section', 'expert', 'hid'), may hold values from -6 to 6
- next_input: bfloat16 [2, 512, 4096], P('section', 'expert', 'hid'), may hold values from -6 to 6
- routes_saved: int32 [2, 512, 2], P('section', 'expert'), may hold values from 0 to 3, all different within a row; in each aligned block of 128 rows (0 to 127, 128 to 255, ..., all dimensions but the last counted through in order) at most 96 rows name the same one
- routes_next: int32 [2, 512, 2], P('section', 'expert'), may hold values from 0 to 3, all different within a row; in each aligned block of 128 rows (0 to 127, 128 to 255, ..., all dimensions but the last counted through in order) at most 96 rows name the same one
- norm_gain: float32 [2, 4096], P('section', 'hid'), may hold values from 0.1 to 1.9
- router: float32 [2, 4096, 4], P('section', 'hid'), may hold values from -0.18 to 0.18
- expert_gate: bfloat16 [2, 4, 4096, 7168], P('section', 'expert', None, 'hid'), may hold values from -0.09375 to 0.09375
- expert_up: bfloat16 [2, 4, 4096, 7168], P('section', 'expert', None, 'hid'), may hold values from -0.09375 to 0.09375
- expert_down: bfloat16 [2, 4, 7168, 4096], P('section', 'expert', 'hid'), may hold values from -0.0625 to 0.0625
Outputs:
- leaving: bfloat16 [2, 512, 4096], P('section', 'expert', 'hid')
- arriving: bfloat16 [2, 512, 4096], P('section', 'expert', 'hid')
Inputs may be any that keep to these rules, and one draw needn't show every extreme that they name: `routes_saved`: A token's two ids differ. In each aligned block of 128 tokens of a section no expert is named by more than 96 tokens, and some block names some expert exactly 96 times. `routes_next`: A token's two ids differ. In each aligned block of 128 tokens of a section no expert is named by more than 96 tokens, and some block names some expert exactly 96 times.
All inputs are finite; a program needn't handle non-finite values.
Results may differ from a plain program's by a relative error of at most 0.0052.
Values may be sent and summed in bfloat16 or wider, within the bound.
A program may use at most 128 MiB of HBM per device.

v0:
```python
import functools

import jax
import jax.numpy as jnp
from jax import lax
from jax.experimental import pallas as pl
from jax.experimental.pallas import tpu as pltpu
from jax.sharding import PartitionSpec as P

EPSILON = 1e-05
F32 = jnp.float32
BF16 = jnp.bfloat16
I32 = jnp.int32
NN = (((1,), (0,)), ((), ()))
NT = (((1,), (1,)), ((), ()))
LANES = 128
A_SLOTS = 3
R_SLOTS = 4
COT, NXT, SAV = 0, 1, 2


def bits_of(count):
    return [1 << bit for bit in range(count.bit_length() - 1)]


def low_bit(number):
    return number & -number


def flip(value, mask, count):
    total = 0
    for bit in bits_of(count):
        own = lax.rem(lax.div(value, bit), 2)
        if isinstance(mask, int):
            got = 1 - own if mask & bit else own
        else:
            other = lax.rem(lax.div(mask, bit), 2)
            got = own + other - 2 * own * other
        total = total + bit * got
    return total


def dot(a, b, dims=NN):
    return lax.dot_general(a, b, dims, preferred_element_type=F32)


def kernel(
    sizes,
    saved_ref, cot_ref, next_ref, routes_ref, gain_ref, table_ref, wg_ref, wu_ref, wd_ref,
    leaving_ref, arriving_ref,
    rows, slots, wa, wr, gh, hid_n, grads, rs_send, rs_recv, own_part, home_send, home,
    stat_send, stat_recv, dots_acc, dots_send, dots_recv, tail_send, tail_recv,
    cols, mixed, there_send, there_recv,
    wa_sem, wr_sem,
    z_send, z_recv, g_send, g_recv, s_send, s_recv, r_send, r_recv,
    b_send, b_recv, d_send, d_recv, t_send, t_recv, y_send, y_recv,
):
    E, H, T, F, D, ffd, cap, tn, tw = sizes
    n_tiles, n_cols = ffd // tn, F // tw
    steps = H * n_cols
    all_rows = E * cap
    sec, me, hi = lax.axis_index("section"), lax.axis_index("expert"), lax.axis_index("hid")
    hid_peer = [flip(hi, m, H) for m in range(H)]
    exp_peer = [flip(me, k, E) for k in range(E)]
    to_send = []
    none = me * 0

    def remote(src, dst, send, recv, e=None, h=None, s=None):
        where = (sec if s is None else s, me if e is None else e, hi if h is None else h)
        return pltpu.make_async_remote_copy(
            src_ref=src, dst_ref=dst, send_sem=send, recv_sem=recv,
            device_id=where, device_id_type=pl.DeviceIdType.MESH,
        )

    def send(build):
        build().start()
        to_send.append(build)

    def a_copies(kind, j, slot):
        if kind == "out":
            m = H - 1 - lax.div(j, n_cols)
            col = pl.multiple_of(flip(hi, m, H) * F + lax.rem(j, n_cols) * tw, tw)
            return [pltpu.make_async_copy(
                wd_ref.at[:, pl.ds(col, tw)], wa.at[slot, 0, pl.ds(0, ffd), pl.ds(0, tw)], wa_sem.at[slot, 0])]
        col = pl.multiple_of(j * tn, tn)
        return [
            pltpu.make_async_copy(w.at[:, pl.ds(col, tn)], wa.at[slot, half, :, pl.ds(0, tn)], wa_sem.at[slot, half])
            for half, w in enumerate((wg_ref, wu_ref))
        ]

    def start_a(g):
        slot = lax.rem(g, A_SLOTS)

        @pl.when((g < n_tiles) | (g >= n_tiles + steps) & (g < 2 * n_tiles + steps))
        def _():
            for copy in a_copies("pair", lax.rem(jnp.where(g < n_tiles, g, g - steps - n_tiles), n_tiles), slot):
                copy.start()

        @pl.when((g >= n_tiles) & (g < n_tiles + steps))
        def _():
            for copy in a_copies("out", g - n_tiles, slot):
                copy.start()

    def gh_copy(j):
        slot = lax.rem(j, R_SLOTS)
        return pltpu.make_async_copy(
            wd_ref.at[pl.ds(pl.multiple_of(j * tn, tn), tn), :], wr.at[slot, pl.ds(0, tn), pl.ds(0, D)],
            wr_sem.at[slot, 0])

    def back_copies(i):
        slot = lax.rem(i, R_SLOTS)
        m = H - 1 - lax.div(i, n_cols)
        row = pl.multiple_of(flip(hi, m, H) * F + lax.rem(i, n_cols) * tw, tw)
        return [
            pltpu.make_async_copy(
                w.at[pl.ds(row, tw), :], wr.at[slot, pl.ds(0, tw), pl.ds(half * ffd, ffd)], wr_sem.at[slot, half])
            for half, w in enumerate((wg_ref, wu_ref))
        ]

    for j in range(min(R_SLOTS - 1, n_tiles)):
        gh_copy(none + j).start()
    for g in range(A_SLOTS - 1):
        for copy in a_copies("pair", none + g, none + g):
            copy.start()

    barrier = pltpu.get_barrier_semaphore()
    partners = [(sec, me, hid_peer[m]) for m in range(1, H)]
    partners += [(sec, exp_peer[k], hi) for k in range(1, E)]
    partners += [(1 - sec, me, hi)]
    for where in partners:
        pl.semaphore_signal(barrier, inc=1, device_id=where, device_id_type=pl.DeviceIdType.MESH)
    lane = lax.broadcasted_iota(I32, (T, LANES), 1)
    gain = gain_ref[...]
    routes = routes_ref[...]
    route_cols = [routes[:, n:n + 1].astype(F32) for n in range(4)]
    spread = jnp.zeros((T, LANES), F32)
    for n in range(4):
        spread = spread + jnp.where(lane == n, route_cols[n], 0.0)
    route_rows = spread.T
    first_i = lax.broadcasted_iota(I32, (T, T), 0)
    second_i = lax.broadcasted_iota(I32, (T, T), 1)
    upper = jnp.where(first_i < second_i, 1.0, 0.0).astype(BF16)
    lower = jnp.where(first_i > second_i, 1.0, 0.0).astype(BF16)
    slot_i = lax.broadcasted_iota(I32, (cap, T), 0).astype(F32)
    lane_f = lane.astype(F32)

    def chosen(base, expert):
        first, second = route_rows[base:base + 1], route_rows[base + 1:base + 2]
        wanted = expert.astype(F32)
        hit = jnp.where(first == wanted, 1.0, 0.0) + jnp.where(second == wanted, 1.0, 0.0)
        rank = dot(jnp.broadcast_to(hit, (16, T)).astype(BF16), upper)[0:1]
        rank = jnp.where(hit > 0.5, rank, -1.0)
        return jnp.where(slot_i == rank, 1.0, 0.0).astype(BF16)

    def put(n, value):
        cols[:, n:n + 1] = value

    for n, base in enumerate((0, 2)):
        hits = jnp.where(lane_f == route_cols[base], 1.0, 0.0) + jnp.where(lane_f == route_cols[base + 1], 1.0, 0.0)
        ranks = dot(lower, hits.astype(BF16))
        for c in range(2):
            route = route_cols[base + c]
            put(16 + 2 * n + c, jnp.sum(jnp.where(lane_f == route, ranks, 0.0), axis=1, keepdims=True))
            put(20 + 2 * n + c, route)

    pl.semaphore_wait(barrier, len(partners))

    def region(tau, expert, feature):
        return rows.at[tau, pl.ds(pl.multiple_of(expert * cap, 16), cap), pl.ds(pl.multiple_of(feature * F, LANES), F)]

    def forward_copy(tau, piece, bit, k):
        part = region(tau, exp_peer[k], hid_peer[piece])
        return remote(part, part, g_send.at[tau, piece + bit, k], g_recv.at[tau, piece + bit, k], h=hid_peer[bit])

    def forward(tau, piece, k):
        for bit in reversed(bits_of(H)):
            if piece == 0 or bit < low_bit(piece):
                send(functools.partial(forward_copy, tau, piece, bit, k))

    def got_piece(tau, piece, k):
        part = region(tau, exp_peer[k], hid_peer[piece])
        remote(part, part, g_send.at[tau, piece, k], g_recv.at[tau, piece, k], h=hid_peer[low_bit(piece)]).wait_recv()

    def dispatch_copy(tau, k):
        return remote(
            slots.at[tau, k - 1], region(tau, me, hi), z_send.at[tau, k], z_recv.at[tau, k], e=exp_peer[k])

    def dispatch(tau, base, tokens):
        for k in list(range(E - 1, 0, -1)) + [0]:
            picked = dot(chosen(base, exp_peer[k]), tokens).astype(BF16)
            if k == 0:
                rows[tau, pl.ds(pl.multiple_of(me * cap, 16), cap), pl.ds(pl.multiple_of(hi * F, LANES), F)] = picked
                forward(tau, 0, 0)
            else:
                slots[tau, k - 1] = picked
                send(functools.partial(dispatch_copy, tau, k))

    def z_event(tau, k):
        part = region(tau, exp_peer[k], hi)
        remote(part, part, z_send.at[tau, k], z_recv.at[tau, k], e=exp_peer[k]).wait_recv()
        forward(tau, 0, k)

    relays = [p for top in reversed(bits_of(H)) if top > 1 for p in range(top, H, 2 * top)]

    def x_event(tau, k):
        for piece in relays:
            got_piece(tau, piece, k)
            forward(tau, piece, k)

    order = list(range(E - 1, 0, -1))

    def gather_events(tau):
        events = [functools.partial(x_event, tau, 0)]
        for k in order:
            events.insert(-1, functools.partial(z_event, tau, k))
            events.append(functools.partial(x_event, tau, k))
        return events

    def complete(tau):
        for piece in range(1, H, 2):
            for k in range(E):
                got_piece(tau, piece, k)

    dispatch(COT, 0, cot_ref[...])

    stats = jnp.zeros((T, LANES), F32)
    for offset, ref in ((0, saved_ref), (16, next_ref)):
        values = ref[...].astype(F32)
        stats = stats + jnp.where(lane == offset, jnp.sum(values * values, axis=1, keepdims=True), 0.0)
        for e in range(E):
            weights = table_ref[e:e + 1, :] * gain
            stats = stats + jnp.where(lane == offset + 1 + e, jnp.sum(values * weights, axis=1, keepdims=True), 0.0)
    stat_send[...] = stats.T[0:32]

    def all_to_hid(src, dst, sent, recv):
        copies = [remote(src, dst.at[m - 1], sent.at[m], recv.at[m], h=hid_peer[m]) for m in range(1, H)]
        for copy in copies:
            send(lambda copy=copy: copy)
        return copies

    stat_copies = all_to_hid(stat_send, stat_recv, s_send, s_recv)
    total = stats.T[0:32]
    for m, copy in enumerate(stat_copies):
        copy.wait_recv()
        total = total + stat_recv[m]
    stats = jnp.concatenate([total, jnp.zeros((LANES - 32, T), F32)], axis=0).T

    def finish_norm(offset, base, ref, keep):
        scale = lax.rsqrt(stats[:, offset:offset + 1] / D + EPSILON)
        first_score = jnp.zeros((T, 1), F32)
        second_score = jnp.zeros((T, 1), F32)
        for e in range(E):
            score = stats[:, offset + 1 + e:offset + 2 + e]
            first_score = first_score + jnp.where(route_cols[base] == e, score, 0.0)
            second_score = second_score + jnp.where(route_cols[base + 1] == e, score, 0.0)
        first, second = first_score * scale, second_score * scale
        put(keep, jax.nn.sigmoid(first - second))
        put(keep + 1, jax.nn.sigmoid(second - first))
        put(keep + 2, scale)
        put(keep + 3, first_score - second_score)
        return (ref[...].astype(F32) * scale * gain).astype(BF16)

    dispatch(NXT, 2, finish_norm(16, 2, next_ref, 4))
    dispatch(SAV, 0, finish_norm(0, 0, saved_ref, 0))

    def reduce_step(which, acc, i):
        m_now, c = H - 1 - lax.div(i, n_cols), lax.rem(i, n_cols)

        @pl.when(m_now == 0)
        def _():
            own_part[which, c] = acc

        for m in range(1, H):
            @pl.when(m_now == m)
            def _():
                value = acc
                for bit in bits_of(low_bit(m) * 2)[:-1]:
                    received(which, m + bit, c)
                    value = value + rs_recv[which, m + bit - 1, c].astype(F32)
                rs_send[which, m - 1, c] = value.astype(BF16)
                reduce_copy(which, m, c).start()

    def reduce_copy(which, m, c):
        return remote(
            rs_send.at[which, m - 1, c], rs_recv.at[which, m - 1, c],
            r_send.at[which, m, c], r_recv.at[which, m, c], h=hid_peer[low_bit(m)])

    def received(which, m, c):
        reduce_copy(which, m, c).wait_recv()

    def home_region(which, expert, c):
        return home.at[which, pl.ds(pl.multiple_of(expert * cap, 16), cap), pl.ds(c * tw, tw)]

    def home_copy(which, k, c):
        return remote(
            home_send.at[which, c, pl.ds(pl.multiple_of(exp_peer[k] * cap, 16), cap)], home_region(which, me, c),
            b_send.at[which, k, c], b_recv.at[which, k, c], e=exp_peer[k])

    def home_event(which, c):
        value = own_part[which, c]
        for bit in bits_of(H):
            received(which, bit, c)
            value = value + rs_recv[which, bit - 1, c].astype(F32)
        home_send[which, c] = value.astype(BF16)
        for k in order:
            send(functools.partial(home_copy, which, k, c))
        mine = pl.ds(pl.multiple_of(me * cap, 16), cap)
        home[which, mine, c * tw:(c + 1) * tw] = home_send[which, c, mine, :]

    def home_wait(which, c):
        for k in order:
            part = home_region(which, exp_peer[k], c)
            remote(part, part, b_send.at[which, k, c], b_recv.at[which, k, c], e=exp_peer[k]).wait_recv()

    wide_i = lax.broadcasted_iota(I32, (T, all_rows), 1).astype(F32)

    def selectors(n):
        picks = []
        for c in range(2):
            rank, route = cols[:, 16 + 2 * n + c:17 + 2 * n + c], cols[:, 20 + 2 * n + c:21 + 2 * n + c]
            picks.append(jnp.where(wide_i == route * cap + rank, 1.0, 0.0).astype(BF16))
        return picks

    def blended(which, n, keep, c, picks):
        part = home[which, :, c * tw:(c + 1) * tw]
        return cols[:, keep:keep + 1] * dot(picks[0], part) + cols[:, keep + 1:keep + 2] * dot(picks[1], part)

    def there_copy(n, height):
        part = pl.ds(n * height, height)
        return remote(there_send.at[part], there_recv.at[part], y_send.at[n], y_recv.at[n], s=1 - sec)

    halves = 2
    half_rows = T // halves

    def forward_out():
        picks = selectors(1)
        for c in range(n_cols):
            home_wait(0, c)
            part = slice(c * tw, (c + 1) * tw)
            value = (next_ref[:, part].astype(F32) + blended(0, 1, 4, c, picks)).astype(BF16)

            @pl.when(sec == 0)
            def _():
                there_send[:, part] = value

            @pl.when(sec == 1)
            def _():
                leaving_ref[:, part] = value

        @pl.when(sec == 0)
        def _():
            for n in range(halves):
                there_copy(n, half_rows).start()

    def run(events, index):
        for at, event in events:
            pl.when(index == at)(event)

    def place(events, spots, limit):
        return [(min(spot, limit - 1), event) for event, spot in zip(events, spots)]

    for event in gather_events(COT):
        event()
    complete(COT)
    next_events = gather_events(NXT)
    early = 4 if E == 4 else len(next_events) // 2
    spots = [(1 + 5 * n // early) for n in range(early)]
    gh_events = place(next_events[:early], spots, n_tiles)

    @pl.loop(0, n_tiles)
    def _(j):
        @pl.when(j + R_SLOTS - 1 < n_tiles)
        def _():
            gh_copy(j + R_SLOTS - 1).start()

        gh_copy(j).wait()
        slot = lax.rem(j, R_SLOTS)
        gh[:, pl.ds(pl.multiple_of(j * tn, tn), tn)] = dot(rows[COT], wr[slot, 0:tn, 0:D], NT)
        run(gh_events, j)

    for i in range(R_SLOTS - 1):
        for copy in back_copies(none + i):
            copy.start()

    for event in next_events[early:]:
        event()
    complete(NXT)

    saved_events = gather_events(SAV)
    late = 1
    count = len(saved_events) - late
    spots = [(n_tiles - 1) * n // max(1, count - 1) for n in range(count)]
    up_events = place(saved_events[:count], spots, n_tiles)

    @pl.loop(0, n_tiles)
    def _(j):
        start_a(j + A_SLOTS - 1)
        slot = lax.rem(j, A_SLOTS)
        for copy in a_copies("pair", j, slot):
            copy.wait()
        gate = dot(rows[NXT], wa[slot, 0, :, 0:tn])
        up = dot(rows[NXT], wa[slot, 1, :, 0:tn])
        hid_n[:, pl.ds(pl.multiple_of(j * tn, tn), tn)] = (gate * jax.nn.sigmoid(gate) * up).astype(BF16)
        run(up_events, j)

    out_events = place(saved_events[count:], [(3 * steps) // 4] * late, steps)

    @pl.loop(0, steps)
    def _(i):
        g = n_tiles + i
        start_a(g + A_SLOTS - 1)
        slot = lax.rem(g, A_SLOTS)
        for copy in a_copies("out", i, slot):
            copy.wait()
        reduce_step(0, dot(hid_n[...], wa[slot, 0, 0:ffd, 0:tw]), i)
        run(out_events, i)

    complete(SAV)

    dots_acc[...] = jnp.zeros_like(dots_acc)
    down_spots = [1 + 2 * c for c in range(n_cols)]
    in_gate = [c for c in range(n_cols) if down_spots[c] < n_tiles - 1]
    gate_events = [(down_spots[c], functools.partial(home_event, 0, c)) for c in in_gate]

    @pl.loop(0, n_tiles)
    def _(j):
        g = n_tiles + steps + j
        start_a(g + A_SLOTS - 1)
        slot = lax.rem(g, A_SLOTS)
        for copy in a_copies("pair", j, slot):
            copy.wait()
        gate = dot(rows[SAV], wa[slot, 0, :, 0:tn])
        up = dot(rows[SAV], wa[slot, 1, :, 0:tn])
        part = pl.ds(pl.multiple_of(j * tn, tn), tn)
        grad = gh[:, part]
        sig = jax.nn.sigmoid(gate)
        silu = gate * sig
        hidden = (silu * up).astype(BF16).astype(F32)
        grads[0, :, part] = (grad * up * (sig * (1.0 + gate * (1.0 - sig)))).astype(BF16)
        grads[1, :, part] = (grad * silu).astype(BF16)
        product = grad * hidden
        partial = product[:, 0:LANES]
        for n in range(1, tn // LANES):
            partial = partial + product[:, n * LANES:(n + 1) * LANES]
        dots_acc[...] += partial
        run(gate_events, j)

    def dots_copy(k):
        return remote(dots_send, dots_recv.at[k - 1], d_send.at[k], d_recv.at[k], e=exp_peer[k])

    dots_send[...] = jnp.broadcast_to(jnp.sum(dots_acc[...].T, axis=0, keepdims=True), (8, all_rows))
    for k in order:
        send(functools.partial(dots_copy, k))

    def dots_event():
        for k in order:
            dots_copy(k).wait_recv()
        gap = jnp.zeros((T, 1), F32)
        for k in range(E):
            row = dots_send[0:1] if k == 0 else dots_recv[k - 1, 0:1]
            expert = exp_peer[k].astype(F32)
            for c, sign in ((0, 1.0), (1, -1.0)):
                rank, route = cols[:, 16 + c:17 + c], cols[:, 20 + c:21 + c]
                spot = jnp.where(route == expert, me.astype(F32) * cap + rank, -1.0)
                gap = gap + sign * jnp.sum(jnp.where(wide_i == spot, row, 0.0), axis=1, keepdims=True)
        put(8, gap)

    late_events = [(1 + 2 * n, functools.partial(home_event, 0, c)) for n, c in enumerate(c for c in range(n_cols) if c not in in_gate)]
    back_events = late_events + [((steps * 5) // 8, dots_event), ((steps * 3) // 4, forward_out)]

    @pl.loop(0, steps)
    def _(i):
        @pl.when(i + R_SLOTS - 1 < steps)
        def _():
            for copy in back_copies(i + R_SLOTS - 1):
                copy.start()

        for copy in back_copies(i):
            copy.wait()
        slot = lax.rem(i, R_SLOTS)
        acc = dot(grads[0], wr[slot, 0:tw, 0:ffd], NT) + dot(grads[1], wr[slot, 0:tw, ffd:2 * ffd], NT)
        reduce_step(1, acc, i)
        run(back_events, i)

    for c in range(n_cols):
        home_event(1, c)
    picks = selectors(0)
    inner = jnp.zeros((T, 1), F32)
    for c in range(n_cols):
        home_wait(1, c)
        part = slice(c * tw, (c + 1) * tw)
        value = blended(1, 0, 0, c, picks) * gain_ref[:, part]
        mixed[:, part] = value
        inner = inner + jnp.sum(value * saved_ref[:, part].astype(F32), axis=1, keepdims=True)
    message = jnp.where(lane == 0, inner, 0.0) + jnp.where(lane == 1, cols[:, 8:9], 0.0)
    message = message.T[0:8]
    tail_send[...] = message
    for m, copy in enumerate(all_to_hid(tail_send, tail_recv, t_send, t_recv)):
        copy.wait_recv()
        message = message + tail_recv[m]
    message = jnp.concatenate([message, jnp.zeros((LANES - 8, T), F32)], axis=0).T
    scale = cols[:, 2:3]
    slope = message[:, 1:2] * cols[:, 0:1] * cols[:, 1:2]
    inner = message[:, 0:1] + slope * cols[:, 3:4]
    pull = scale * scale * scale * (inner / D)
    for n in range(halves):
        part = slice(n * half_rows, (n + 1) * half_rows)
        lean = jnp.zeros((half_rows, F), F32)
        for e in range(E):
            sign = jnp.where(cols[part, 20:21] == e, 1.0, 0.0) - jnp.where(cols[part, 21:22] == e, 1.0, 0.0)
            lean = lean + sign * table_ref[e:e + 1, :]
        grad = mixed[part, :] + slope[part] * lean * gain
        value = (
            cot_ref[part, :].astype(F32) + scale[part] * grad - saved_ref[part, :].astype(F32) * pull[part]
        ).astype(BF16)

        @pl.when(sec == 0)
        def _():
            leaving_ref[part, :] = value

        @pl.when(sec == 1)
        def _():
            there_send[part, :] = value
            there_copy(n, half_rows).start()

    for n in range(halves):
        copy = there_copy(n, half_rows)
        copy.wait_recv()
        arriving_ref[n * half_rows:(n + 1) * half_rows, :] = there_recv[n * half_rows:(n + 1) * half_rows, :]

    for build in to_send:
        build().wait_send()
    for which in range(2):
        for m in range(1, H):
            for c in range(n_cols):
                reduce_copy(which, m, c).wait_send()
    for n in range(halves):
        there_copy(n, half_rows).wait_send()


def per_device(
    saved_input,
    cotangent,
    next_input,
    routes_saved,
    routes_next,
    norm_gain,
    router,
    expert_gate,
    expert_up,
    expert_down,
):
    E, H = lax.axis_size("expert"), lax.axis_size("hid")
    T, F = saved_input.shape[1:]
    D, ffd = expert_gate.shape[2:]
    cap = 3 * T // router.shape[2]
    tn = 2 * LANES if ffd % (2 * LANES) == 0 else LANES
    tw = 2 * LANES if F % (2 * LANES) == 0 else LANES
    n_cols, all_rows = F // tw, E * cap
    deep, wide = max(tn, tw), max(D, 2 * ffd)
    routes = jnp.concatenate([routes_saved[0], routes_next[0]], axis=1)
    vmem = pl.BlockSpec(memory_space=pltpu.VMEM)
    hbm = pl.BlockSpec(memory_space=pl.ANY)
    dma = pltpu.SemaphoreType.DMA
    block = jax.ShapeDtypeStruct((T, F), BF16)
    scratch = [
        pltpu.VMEM((3, all_rows, D), BF16),
        pltpu.VMEM((3, E - 1, cap, F), BF16),
        pltpu.VMEM((A_SLOTS, 2, D, deep), BF16),
        pltpu.VMEM((R_SLOTS, deep, wide), BF16),
        pltpu.VMEM((all_rows, ffd), F32),
        pltpu.VMEM((all_rows, ffd), BF16),
        pltpu.VMEM((2, all_rows, ffd), BF16),
        pltpu.VMEM((2, H - 1, n_cols, all_rows, tw), BF16),
        pltpu.VMEM((2, H - 1, n_cols, all_rows, tw), BF16),
        pltpu.VMEM((2, n_cols, all_rows, tw), F32),
        pltpu.VMEM((2, n_cols, all_rows, tw), BF16),
        pltpu.VMEM((2, all_rows, F), BF16),
        pltpu.VMEM((32, T), F32),
        pltpu.VMEM((H - 1, 32, T), F32),
        pltpu.VMEM((all_rows, LANES), F32),
        pltpu.VMEM((8, all_rows), F32),
        pltpu.VMEM((E - 1, 8, all_rows), F32),
        pltpu.VMEM((8, T), F32),
        pltpu.VMEM((H - 1, 8, T), F32),
        pltpu.VMEM((T, LANES), F32),
        pltpu.VMEM((T, F), F32),
        pltpu.VMEM((T, F), BF16),
        pltpu.VMEM((T, F), BF16),
        dma((A_SLOTS, 2)),
        dma((R_SLOTS, 2)),
        dma((3, E)),
        dma((3, E)),
        dma((3, H, E)),
        dma((3, H, E)),
        dma((H,)),
        dma((H,)),
        dma((2, H, n_cols)),
        dma((2, H, n_cols)),
        dma((2, E, n_cols)),
        dma((2, E, n_cols)),
        dma((E,)),
        dma((E,)),
        dma((H,)),
        dma((H,)),
        dma((2,)),
        dma((2,)),
    ]
    leaving, arriving = pl.pallas_call(
        functools.partial(kernel, (E, H, T, F, D, ffd, cap, tn, tw)),
        out_shape=(block, block),
        in_specs=[vmem] * 6 + [hbm] * 3,
        out_specs=(vmem, vmem),
        scratch_shapes=scratch,
        compiler_params=pltpu.CompilerParams(
            collective_id=0, has_side_effects=True, vmem_limit_bytes=67043328
        ),
        name="relay",
    )(
        saved_input[0], cotangent[0], next_input[0], routes, norm_gain, router[0].T,
        expert_gate[0, 0], expert_up[0, 0], expert_down[0, 0],
    )
    return (leaving[None], arriving[None])


def solution(mesh):
    placed = (
        P("section", "expert", "hid"),
        P("section", "expert", "hid"),
        P("section", "expert", "hid"),
        P("section", "expert", None),
        P("section", "expert", None),
        P("section", "hid"),
        P("section", "hid", None),
        P("section", "expert", None, "hid"),
        P("section", "expert", None, "hid"),
        P("section", "expert", "hid", None),
    )
    return jax.shard_map(
        per_device,
        mesh=mesh,
        in_specs=placed,
        out_specs=(P("section", "expert", "hid"), P("section", "expert", "hid")),
        check_vma=False,
    )
```

profile of v0, /device:TPU:0, one launch (start us, length us, event | category | flops | bytes accessed | tf_op | source)
XLA Modules:
  0.0 156.7 jit_solution(14864386845373706021)
XLA Ops:
  0.6 0.7 pad_add_fusion
  1.3 0.7 copy.14.routes_ref
  2.1 151.3 %relay.1 = (bf16[128,1024]{1,0:T(8,128)(2,1)}, bf16[128,1024]{1,0:T(8,128)(2,1)}) custom-call(bf16[128,1024]{1,0:T(8,128)(2,1)} %bitcast.16, bf16[128,1024]{1,0:T(8,128)(2,1)} %bitcast.17, bf16[128,1024]{1,0:T(8,128)(2,1)} %bitcast.18, s32[128,4]{1,0:T(8,128)} %copy.14.routes_ref, f32[1,1024]{1,0:T(1,128)} %gain_ref.1, f32[4,1024]{1,0:T(4,128)} %bitcast.21, ...), custom_call_target="tpu_custom_call" | custom-call | tf_op jit(solution)/shard_map/relay/pallas_call | solution.py:609
  153.4 1.7 %copy.17 = bf16[1,128,1024]{2,1,0:T(8,128)(2,1)} copy(bf16[1,128,1024]{2,1,0:T(8,128)(2,1)} %bitcast.20) | data formatting | bytes 524288
  155.0 1.7 %copy.18 = bf16[1,128,1024]{2,1,0:T(8,128)(2,1)} copy(bf16[1,128,1024]{2,1,0:T(8,128)(2,1)} %bitcast.19) | data formatting | bytes 524288
where the time goes:
time: 157 us
  Pallas kernels  151 us (96%)
  local copies, waits for them, and re-layouts  4.08 us (3%)
    pallas_call x1, Pallas kernels, per_device(): pl.pallas_call(functools.partial(kernel, (E, H, T, F, D, ffd, cap, tn, tw...  151 us
    unnamed x2, local copies, waits for them, and re-layouts  3.34 us

commit v1 on v0

--- a/solution.py
+++ b/solution.py
@@ -46,14 +46,14 @@
 
 def kernel(
     sizes,
-    saved_ref, cot_ref, next_ref, routes_ref, gain_ref, table_ref, wg_ref, wu_ref, wd_ref,
-    leaving_ref, arriving_ref,
+    saved_ref, cot_ref, next_ref, pair_saved_ref, pair_next_ref, gain_ref, table_ref, wg_ref, wu_ref, wd_ref,
+    out_ref,
     rows, slots, wa, wr, gh, hid_n, grads, rs_send, rs_recv, own_part, home_send, home,
     stat_send, stat_recv, dots_acc, dots_send, dots_recv, tail_send, tail_recv,
-    cols, mixed, there_send, there_recv,
+    cols, mixed, there_send, there_recv, far_cot, far_saved, far_value, far_gain, far_table, far_cols, far_tail,
     wa_sem, wr_sem,
     z_send, z_recv, g_send, g_recv, s_send, s_recv, r_send, r_recv,
-    b_send, b_recv, d_send, d_recv, t_send, t_recv, y_send, y_recv,
+    b_send, b_recv, d_send, d_recv, t_send, t_recv, y_send, y_recv, e_send, e_recv, f_send, f_recv,
 ):
     E, H, T, F, D, ffd, cap, tn, tw = sizes
     n_tiles, n_cols = ffd // tn, F // tw
@@ -76,27 +76,37 @@
         build().start()
         to_send.append(build)
 
+    def place_of(i):
+        at = lax.rem(i, H)
+        return H - 1 - 2 * at + lax.div(at, H // 2) * (H - 1), lax.div(i, H)
+
     def a_copies(kind, j, slot):
         if kind == "out":
-            m = H - 1 - lax.div(j, n_cols)
-            col = pl.multiple_of(flip(hi, m, H) * F + lax.rem(j, n_cols) * tw, tw)
-            return [pltpu.make_async_copy(
-                wd_ref.at[:, pl.ds(col, tw)], wa.at[slot, 0, pl.ds(0, ffd), pl.ds(0, tw)], wa_sem.at[slot, 0])]
+            copies = []
+            for half in range(2):
+                m, c = place_of(2 * j + half)
+                col = pl.multiple_of(flip(hi, m, H) * F + c * tw, tw)
+                copies.append(pltpu.make_async_copy(
+                    wd_ref.at[:, pl.ds(col, tw)], wa.at[slot, half, pl.ds(0, ffd), pl.ds(0, tw)],
+                    wa_sem.at[slot, half]))
+            return copies
         col = pl.multiple_of(j * tn, tn)
         return [
             pltpu.make_async_copy(w.at[:, pl.ds(col, tn)], wa.at[slot, half, :, pl.ds(0, tn)], wa_sem.at[slot, half])
             for half, w in enumerate((wg_ref, wu_ref))
         ]
 
+    out_items = steps // 2
+
     def start_a(g):
         slot = lax.rem(g, A_SLOTS)
 
-        @pl.when((g < n_tiles) | (g >= n_tiles + steps) & (g < 2 * n_tiles + steps))
+        @pl.when((g < n_tiles) | (g >= n_tiles + out_items) & (g < 2 * n_tiles + out_items))
         def _():
-            for copy in a_copies("pair", lax.rem(jnp.where(g < n_tiles, g, g - steps - n_tiles), n_tiles), slot):
+            for copy in a_copies("pair", lax.rem(jnp.where(g < n_tiles, g, g - out_items - n_tiles), n_tiles), slot):
                 copy.start()
 
-        @pl.when((g >= n_tiles) & (g < n_tiles + steps))
+        @pl.when((g >= n_tiles) & (g < n_tiles + out_items))
         def _():
             for copy in a_copies("out", g - n_tiles, slot):
                 copy.start()
@@ -109,8 +119,8 @@
 
     def back_copies(i):
         slot = lax.rem(i, R_SLOTS)
-        m = H - 1 - lax.div(i, n_cols)
-        row = pl.multiple_of(flip(hi, m, H) * F + lax.rem(i, n_cols) * tw, tw)
+        m, c = place_of(i)
+        row = pl.multiple_of(flip(hi, m, H) * F + c * tw, tw)
         return [
             pltpu.make_async_copy(
                 w.at[pl.ds(row, tw), :], wr.at[slot, pl.ds(0, tw), pl.ds(half * ffd, ffd)], wr_sem.at[slot, half])
@@ -126,17 +136,15 @@
     barrier = pltpu.get_barrier_semaphore()
     partners = [(sec, me, hid_peer[m]) for m in range(1, H)]
     partners += [(sec, exp_peer[k], hi) for k in range(1, E)]
-    partners += [(1 - sec, me, hi)]
+    partners += [(1 - sec, me, hid_peer[m]) for m in range(H)]
     for where in partners:
         pl.semaphore_signal(barrier, inc=1, device_id=where, device_id_type=pl.DeviceIdType.MESH)
     lane = lax.broadcasted_iota(I32, (T, LANES), 1)
     gain = gain_ref[...]
-    routes = routes_ref[...]
-    route_cols = [routes[:, n:n + 1].astype(F32) for n in range(4)]
-    spread = jnp.zeros((T, LANES), F32)
-    for n in range(4):
-        spread = spread + jnp.where(lane == n, route_cols[n], 0.0)
-    route_rows = spread.T
+    route_rows = jnp.concatenate(
+        [pair_saved_ref[...].astype(F32), pair_next_ref[...].astype(F32), jnp.zeros((LANES - 4, T), F32)], axis=0)
+    spread = route_rows.T
+    route_cols = [spread[:, n:n + 1] for n in range(4)]
     first_i = lax.broadcasted_iota(I32, (T, T), 0)
     second_i = lax.broadcasted_iota(I32, (T, T), 1)
     upper = jnp.where(first_i < second_i, 1.0, 0.0).astype(BF16)
@@ -185,12 +193,13 @@
         return remote(
             slots.at[tau, k - 1], region(tau, me, hi), z_send.at[tau, k], z_recv.at[tau, k], e=exp_peer[k])
 
-    def dispatch(tau, base, tokens):
+    def dispatch(tau, base, tokens, onward):
         for k in list(range(E - 1, 0, -1)) + [0]:
             picked = dot(chosen(base, exp_peer[k]), tokens).astype(BF16)
             if k == 0:
                 rows[tau, pl.ds(pl.multiple_of(me * cap, 16), cap), pl.ds(pl.multiple_of(hi * F, LANES), F)] = picked
-                forward(tau, 0, 0)
+                if onward:
+                    forward(tau, 0, 0)
             else:
                 slots[tau, k - 1] = picked
                 send(functools.partial(dispatch_copy, tau, k))
@@ -220,8 +229,6 @@
         for piece in range(1, H, 2):
             for k in range(E):
                 got_piece(tau, piece, k)
-
-    dispatch(COT, 0, cot_ref[...])
 
     stats = jnp.zeros((T, LANES), F32)
     for offset, ref in ((0, saved_ref), (16, next_ref)):
@@ -239,6 +246,9 @@
         return copies
 
     stat_copies = all_to_hid(stat_send, stat_recv, s_send, s_recv)
+
+    dispatch(COT, 0, cot_ref[...], True)
+
     total = stats.T[0:32]
     for m, copy in enumerate(stat_copies):
         copy.wait_recv()
@@ -260,11 +270,26 @@
         put(keep + 3, first_score - second_score)
         return (ref[...].astype(F32) * scale * gain).astype(BF16)
 
-    dispatch(NXT, 2, finish_norm(16, 2, next_ref, 4))
-    dispatch(SAV, 0, finish_norm(0, 0, saved_ref, 0))
+    dispatch(NXT, 2, finish_norm(16, 2, next_ref, 4), False)
+    dispatch(SAV, 0, finish_norm(0, 0, saved_ref, 0), False)
+
+    far = [(cot_ref, far_cot), (saved_ref, far_saved), (gain_ref, far_gain), (table_ref, far_table), (cols, far_cols)]
+
+    def far_copy(n):
+        return remote(far[n][0], far[n][1], e_send.at[n], e_recv.at[n], s=1 - sec)
+
+    def far_value_copy(c):
+        part = pl.ds(c * tw, tw)
+        n = len(far) + c
+        return remote(there_send.at[:, part], far_value.at[:, part], e_send.at[n], e_recv.at[n], s=1 - sec)
+
+    @pl.when(sec == 1)
+    def _():
+        for n in range(len(far)):
+            far_copy(n).start()
 
     def reduce_step(which, acc, i):
-        m_now, c = H - 1 - lax.div(i, n_cols), lax.rem(i, n_cols)
+        m_now, c = place_of(i)
 
         @pl.when(m_now == 0)
         def _():
@@ -345,7 +370,7 @@
 
             @pl.when(sec == 1)
             def _():
-                leaving_ref[:, part] = value
+                out_ref[0, :, part] = value
 
         @pl.when(sec == 0)
         def _():
@@ -361,6 +386,7 @@
 
     for event in gather_events(COT):
         event()
+    forward(NXT, 0, 0)
     complete(COT)
     next_events = gather_events(NXT)
     early = 4 if E == 4 else len(next_events) // 2
@@ -384,6 +410,7 @@
 
     for event in next_events[early:]:
         event()
+    forward(SAV, 0, 0)
     complete(NXT)
 
     saved_events = gather_events(SAV)
@@ -403,16 +430,16 @@
         hid_n[:, pl.ds(pl.multiple_of(j * tn, tn), tn)] = (gate * jax.nn.sigmoid(gate) * up).astype(BF16)
         run(up_events, j)
 
-    out_events = place(saved_events[count:], [(3 * steps) // 4] * late, steps)
-
-    @pl.loop(0, steps)
+    out_events = place(saved_events[count:], [(3 * out_items) // 4] * late, out_items)
+
+    @pl.loop(0, out_items)
     def _(i):
         g = n_tiles + i
         start_a(g + A_SLOTS - 1)
         slot = lax.rem(g, A_SLOTS)
-        for copy in a_copies("out", i, slot):
+        for half, copy in enumerate(a_copies("out", i, slot)):
             copy.wait()
-        reduce_step(0, dot(hid_n[...], wa[slot, 0, 0:ffd, 0:tw]), i)
+            reduce_step(0, dot(hid_n[...], wa[slot, half, 0:ffd, 0:tw]), 2 * i + half)
         run(out_events, i)
 
     complete(SAV)
@@ -424,7 +451,7 @@
 
     @pl.loop(0, n_tiles)
     def _(j):
-        g = n_tiles + steps + j
+        g = n_tiles + out_items + j
         start_a(g + A_SLOTS - 1)
         slot = lax.rem(g, A_SLOTS)
         for copy in a_copies("pair", j, slot):
@@ -463,10 +490,12 @@
                 rank, route = cols[:, 16 + c:17 + c], cols[:, 20 + c:21 + c]
                 spot = jnp.where(route == expert, me.astype(F32) * cap + rank, -1.0)
                 gap = gap + sign * jnp.sum(jnp.where(wide_i == spot, row, 0.0), axis=1, keepdims=True)
-        put(8, gap)
+        dots_acc[0:T, 0:1] = gap
 
     late_events = [(1 + 2 * n, functools.partial(home_event, 0, c)) for n, c in enumerate(c for c in range(n_cols) if c not in in_gate)]
-    back_events = late_events + [((steps * 5) // 8, dots_event), ((steps * 3) // 4, forward_out)]
+    soon = [c for c in range(n_cols) if H * (c + 2) - 1 < steps]
+    back_events = late_events + [(H * (c + 2) - 1, functools.partial(home_event, 1, c)) for c in soon]
+    back_events += [((steps * 5) // 8, dots_event), ((steps * 3) // 4, forward_out)]
 
     @pl.loop(0, steps)
     def _(i):
@@ -483,7 +512,8 @@
         run(back_events, i)
 
     for c in range(n_cols):
-        home_event(1, c)
+        if c not in soon:
+            home_event(1, c)
     picks = selectors(0)
     inner = jnp.zeros((T, 1), F32)
     for c in range(n_cols):
@@ -491,42 +521,76 @@
         part = slice(c * tw, (c + 1) * tw)
         value = blended(1, 0, 0, c, picks) * gain_ref[:, part]
         mixed[:, part] = value
+
+        @pl.when(sec == 1)
+        def _():
+            there_send[:, part] = value.astype(BF16)
+            far_value_copy(c).start()
+
         inner = inner + jnp.sum(value * saved_ref[:, part].astype(F32), axis=1, keepdims=True)
-    message = jnp.where(lane == 0, inner, 0.0) + jnp.where(lane == 1, cols[:, 8:9], 0.0)
+    message = jnp.where(lane == 0, inner, 0.0) + jnp.where(lane == 1, dots_acc[0:T, 0:1], 0.0)
     message = message.T[0:8]
     tail_send[...] = message
-    for m, copy in enumerate(all_to_hid(tail_send, tail_recv, t_send, t_recv)):
-        copy.wait_recv()
-        message = message + tail_recv[m]
-    message = jnp.concatenate([message, jnp.zeros((LANES - 8, T), F32)], axis=0).T
-    scale = cols[:, 2:3]
-    slope = message[:, 1:2] * cols[:, 0:1] * cols[:, 1:2]
-    inner = message[:, 0:1] + slope * cols[:, 3:4]
-    pull = scale * scale * scale * (inner / D)
-    for n in range(halves):
-        part = slice(n * half_rows, (n + 1) * half_rows)
-        lean = jnp.zeros((half_rows, F), F32)
-        for e in range(E):
-            sign = jnp.where(cols[part, 20:21] == e, 1.0, 0.0) - jnp.where(cols[part, 21:22] == e, 1.0, 0.0)
-            lean = lean + sign * table_ref[e:e + 1, :]
-        grad = mixed[part, :] + slope[part] * lean * gain
-        value = (
-            cot_ref[part, :].astype(F32) + scale[part] * grad - saved_ref[part, :].astype(F32) * pull[part]
-        ).astype(BF16)
-
-        @pl.when(sec == 0)
-        def _():
-            leaving_ref[part, :] = value
-
-        @pl.when(sec == 1)
-        def _():
-            there_send[part, :] = value
-            there_copy(n, half_rows).start()
-
-    for n in range(halves):
-        copy = there_copy(n, half_rows)
-        copy.wait_recv()
-        arriving_ref[n * half_rows:(n + 1) * half_rows, :] = there_recv[n * half_rows:(n + 1) * half_rows, :]
+
+    def tail_copy(m):
+        return remote(tail_send, tail_recv.at[m - 1], t_send.at[m], t_recv.at[m], h=hid_peer[m])
+
+    def far_tail_copy(m):
+        return remote(tail_send, far_tail.at[m], f_send.at[m], f_recv.at[m], h=hid_peer[m], s=1 - sec)
+
+    def input_gradient(message, cot, saved, value_of, gains, table, kept, place_in):
+        message = jnp.concatenate([message, jnp.zeros((LANES - 8, T), F32)], axis=0).T
+        scale = kept[:, 2:3]
+        slope = message[:, 1:2] * kept[:, 0:1] * kept[:, 1:2]
+        inner = message[:, 0:1] + slope * kept[:, 3:4]
+        pull = scale * scale * scale * (inner / D)
+        for n in range(halves):
+            part = slice(n * half_rows, (n + 1) * half_rows)
+            lean = jnp.zeros((half_rows, F), F32)
+            for e in range(E):
+                sign = jnp.where(kept[part, 20:21] == e, 1.0, 0.0) - jnp.where(kept[part, 21:22] == e, 1.0, 0.0)
+                lean = lean + sign * table[e:e + 1, :]
+            grad = value_of[part, :].astype(F32) + slope[part] * lean * gains[...]
+            out_ref[place_in, part, :] = (
+                cot[part, :].astype(F32) + scale[part] * grad - saved[part, :].astype(F32) * pull[part]
+            ).astype(BF16)
+
+    @pl.when(sec == 1)
+    def _():
+        for m in range(H):
+            far_tail_copy(m).start()
+        for n in range(halves):
+            there_copy(n, half_rows).wait_recv()
+        out_ref[1] = there_recv[...]
+        for n in range(len(far)):
+            far_copy(n).wait_send()
+        for c in range(n_cols):
+            far_value_copy(c).wait_send()
+        for m in range(H):
+            far_tail_copy(m).wait_send()
+
+    @pl.when(sec == 0)
+    def _():
+        for m in range(1, H):
+            tail_copy(m).start()
+        total = message
+        for m in range(1, H):
+            tail_copy(m).wait_recv()
+            total = total + tail_recv[m - 1]
+        input_gradient(total, cot_ref, saved_ref, mixed, gain_ref, table_ref, cols, 0)
+        for n in range(len(far)):
+            far_copy(n).wait_recv()
+        for c in range(n_cols):
+            far_value_copy(c).wait_recv()
+        total = jnp.zeros((8, T), F32)
+        for m in range(H):
+            far_tail_copy(m).wait_recv()
+            total = total + far_tail[m]
+        input_gradient(total, far_cot, far_saved, far_value, far_gain, far_table, far_cols, 1)
+        for m in range(1, H):
+            tail_copy(m).wait_send()
+        for n in range(halves):
+            there_copy(n, half_rows).wait_send()
 
     for build in to_send:
         build().wait_send()
@@ -534,8 +598,6 @@
         for m in range(1, H):
             for c in range(n_cols):
                 reduce_copy(which, m, c).wait_send()
-    for n in range(halves):
-        there_copy(n, half_rows).wait_send()
 
 
 def per_device(
@@ -558,11 +620,9 @@
     tw = 2 * LANES if F % (2 * LANES) == 0 else LANES
     n_cols, all_rows = F // tw, E * cap
     deep, wide = max(tn, tw), max(D, 2 * ffd)
-    routes = jnp.concatenate([routes_saved[0], routes_next[0]], axis=1)
     vmem = pl.BlockSpec(memory_space=pltpu.VMEM)
     hbm = pl.BlockSpec(memory_space=pl.ANY)
     dma = pltpu.SemaphoreType.DMA
-    block = jax.ShapeDtypeStruct((T, F), BF16)
     scratch = [
         pltpu.VMEM((3, all_rows, D), BF16),
         pltpu.VMEM((3, E - 1, cap, F), BF16),
@@ -587,6 +647,13 @@
         pltpu.VMEM((T, F), F32),
         pltpu.VMEM((T, F), BF16),
         pltpu.VMEM((T, F), BF16),
+        pltpu.VMEM((T, F), BF16),
+        pltpu.VMEM((T, F), BF16),
+        pltpu.VMEM((T, F), BF16),
+        pltpu.VMEM((1, F), F32),
+        pltpu.VMEM((E, F), F32),
+        pltpu.VMEM((T, LANES), F32),
+        pltpu.VMEM((H, 8, T), F32),
         dma((A_SLOTS, 2)),
         dma((R_SLOTS, 2)),
         dma((3, E)),
@@ -605,22 +672,26 @@
         dma((H,)),
         dma((2,)),
         dma((2,)),
+        dma((5 + n_cols,)),
+        dma((5 + n_cols,)),
+        dma((H,)),
+        dma((H,)),
     ]
-    leaving, arriving = pl.pallas_call(
+    result = pl.pallas_call(
         functools.partial(kernel, (E, H, T, F, D, ffd, cap, tn, tw)),
-        out_shape=(block, block),
-        in_specs=[vmem] * 6 + [hbm] * 3,
-        out_specs=(vmem, vmem),
+        out_shape=jax.ShapeDtypeStruct((2, T, F), BF16),
+        in_specs=[vmem] * 7 + [hbm] * 3,
+        out_specs=vmem,
         scratch_shapes=scratch,
         compiler_params=pltpu.CompilerParams(
             collective_id=0, has_side_effects=True, vmem_limit_bytes=67043328
         ),
         name="relay",
     )(
-        saved_input[0], cotangent[0], next_input[0], routes, norm_gain, router[0].T,
+        saved_input[0], cotangent[0], next_input[0], routes_saved[0].T, routes_next[0].T, norm_gain, router[0].T,
         expert_gate[0, 0], expert_up[0, 0], expert_down[0, 0],
     )
-    return (leaving[None], arriving[None])
+    return (result[0:1], result[1:2])
 
 
 def solution(mesh):

time: 157 us -> 149 us (0.949)
  Pallas kernels: 151 us -> 147 us
  local copies, waits for them, and re-layouts: 4.08 us -> 1.85 us
    pallas_call x1, Pallas kernels: 151 us -> 147 us  [per_device(): pl.pallas_call(functools.partial(kernel, (E, H, T, F, D, ffd, cap, tn, tw...]
    unnamed x2 -> x0, local copies, waits for them, and re-layouts: 3.34 us -> none
    slice x0 -> x1, local copies, waits for them, and re-layouts: none -> 1.85 us  [per_device(): return (result[0:1], result[1:2])]
where the time goes in v1:
time: 149 us
  Pallas kernels  147 us (99%)
  local copies, waits for them, and re-layouts  1.85 us (1%)
    pallas_call x1, Pallas kernels, per_device(): pl.pallas_call(functools.partial(kernel, (E, H, T, F, D, ffd, cap, tn, tw...  147 us

profile of v1, /device:TPU:0, one launch (start us, length us, event | category | flops | bytes accessed | tf_op | source)
XLA Modules:
  0.0 149.1 jit_solution(18000089620021983014)
XLA Ops:
  0.6 146.6 %relay.1 = bf16[2,128,1024]{2,1,0:T(8,128)(2,1)} custom-call(bf16[128,1024]{1,0:T(8,128)(2,1)} %bitcast.18, bf16[128,1024]{1,0:T(8,128)(2,1)} %bitcast.19, bf16[128,1024]{1,0:T(8,128)(2,1)} %bitcast.20, s32[2,128]{1,0:T(2,128)} %bitcast.22, s32[2,128]{1,0:T(2,128)} %bitcast.23, f32[1,1024]{1,0:T(1,128)} %gain_ref.1, f32[4,1024]{1,0:T(4,128)} %bitcast.21, ...), custom_call_target="tpu_custom_call" | custom-call | tf_op jit(solution)/shard_map/relay/pallas_call | solution.py:680
  147.2 1.9 %fusion = (bf16[1,128,1024]{2,1,0:T(8,128)(2,1)}, bf16[1,128,1024]{2,1,0:T(8,128)(2,1)}) fusion(bf16[2,128,1024]{2,1,0:T(8,128)(2,1)} %relay.1), kind=kLoop, calls=%fused_computation | loop fusion | bytes 1048576 | tf_op jit(solution)/shard_map/slice | solution.py:694

commit v2 on v1

--- a/solution.py
+++ b/solution.py
@@ -76,23 +76,24 @@
         build().start()
         to_send.append(build)
 
-    def place_of(i):
+    def place_of(i, kind):
+        if kind == "out":
+            return H - 1 - lax.div(i, n_cols // 2), lax.rem(i, n_cols // 2)
         at = lax.rem(i, H)
         return H - 1 - 2 * at + lax.div(at, H // 2) * (H - 1), lax.div(i, H)
 
+    def out_copy(i, slot):
+        m, c = place_of(i, "out")
+        col = pl.multiple_of(flip(hi, m, H) * F + c * 2 * tw, 2 * tw)
+        return pltpu.make_async_copy(
+            wd_ref.at[:, pl.ds(col, 2 * tw)], wa.at[slot, pl.ds(0, ffd), pl.ds(0, 2 * tw)], wa_sem.at[slot, 0])
+
     def a_copies(kind, j, slot):
         if kind == "out":
-            copies = []
-            for half in range(2):
-                m, c = place_of(2 * j + half)
-                col = pl.multiple_of(flip(hi, m, H) * F + c * tw, tw)
-                copies.append(pltpu.make_async_copy(
-                    wd_ref.at[:, pl.ds(col, tw)], wa.at[slot, half, pl.ds(0, ffd), pl.ds(0, tw)],
-                    wa_sem.at[slot, half]))
-            return copies
+            return [out_copy(j, slot)]
         col = pl.multiple_of(j * tn, tn)
         return [
-            pltpu.make_async_copy(w.at[:, pl.ds(col, tn)], wa.at[slot, half, :, pl.ds(0, tn)], wa_sem.at[slot, half])
+            pltpu.make_async_copy(w.at[:, pl.ds(col, tn)], wa.at[slot, :, pl.ds(half * tn, tn)], wa_sem.at[slot, half])
             for half, w in enumerate((wg_ref, wu_ref))
         ]
 
@@ -119,7 +120,7 @@
 
     def back_copies(i):
         slot = lax.rem(i, R_SLOTS)
-        m, c = place_of(i)
+        m, c = place_of(i, "back")
         row = pl.multiple_of(flip(hi, m, H) * F + c * tw, tw)
         return [
             pltpu.make_async_copy(
@@ -173,6 +174,23 @@
 
     pl.semaphore_wait(barrier, len(partners))
 
+    order = list(range(E - 1, 0, -1))
+    inner = flip(lax.rem(me, 2), lax.rem(lax.div(me, 2), 2), 2)
+    first_sends = ([1, 3, 2], [1, 3, 2]) if E == 4 else (order, order)
+    late_send = None
+    arrivals = ([1, 3, 2], [1, 3, 2]) if E == 4 else (order, order)
+
+    def by_class(build):
+        if E != 4:
+            build(0)
+            return
+        for kind in range(2):
+            pl.when(inner == kind)(functools.partial(build, kind))
+
+    def first_wave(tau):
+        by_class(lambda kind: [dispatch_copy(tau, k).start() for k in first_sends[kind]] and None)
+
+
     def region(tau, expert, feature):
         return rows.at[tau, pl.ds(pl.multiple_of(expert * cap, 16), cap), pl.ds(pl.multiple_of(feature * F, LANES), F)]
 
@@ -180,10 +198,15 @@
         part = region(tau, exp_peer[k], hid_peer[piece])
         return remote(part, part, g_send.at[tau, piece + bit, k], g_recv.at[tau, piece + bit, k], h=hid_peer[bit])
 
-    def forward(tau, piece, k):
-        for bit in reversed(bits_of(H)):
-            if piece == 0 or bit < low_bit(piece):
-                send(functools.partial(forward_copy, tau, piece, bit, k))
+    def forwards(tau, piece, k):
+        return [
+            functools.partial(forward_copy, tau, piece, bit, k)
+            for bit in reversed(bits_of(H)) if piece == 0 or bit < low_bit(piece)
+        ]
+
+    def forward(tau, k):
+        for build in forwards(tau, 0, k):
+            build().start()
 
     def got_piece(tau, piece, k):
         part = region(tau, exp_peer[k], hid_peer[piece])
@@ -193,36 +216,50 @@
         return remote(
             slots.at[tau, k - 1], region(tau, me, hi), z_send.at[tau, k], z_recv.at[tau, k], e=exp_peer[k])
 
-    def dispatch(tau, base, tokens, onward):
-        for k in list(range(E - 1, 0, -1)) + [0]:
+    def dispatch(tau, base, tokens):
+        for k in order + [0]:
             picked = dot(chosen(base, exp_peer[k]), tokens).astype(BF16)
             if k == 0:
                 rows[tau, pl.ds(pl.multiple_of(me * cap, 16), cap), pl.ds(pl.multiple_of(hi * F, LANES), F)] = picked
-                if onward:
-                    forward(tau, 0, 0)
             else:
                 slots[tau, k - 1] = picked
-                send(functools.partial(dispatch_copy, tau, k))
-
-    def z_event(tau, k):
-        part = region(tau, exp_peer[k], hi)
-        remote(part, part, z_send.at[tau, k], z_recv.at[tau, k], e=exp_peer[k]).wait_recv()
-        forward(tau, 0, k)
+
+    def z_event(tau, n):
+        def take(kind):
+            k = arrivals[kind][n]
+            part = region(tau, exp_peer[k], hi)
+            remote(part, part, z_send.at[tau, k], z_recv.at[tau, k], e=exp_peer[k]).wait_recv()
+            for build in forwards(tau, 0, k):
+                build().start()
+            if n == 0 and kind == 1 and late_send:
+                dispatch_copy(tau, late_send).start()
+            if tau < SAV and n == E - 2:
+                for k in first_sends[kind]:
+                    dispatch_copy(tau + 1, k).start()
+
+        by_class(take)
+        if tau < SAV and n == 0:
+            forward(tau + 1, 0)
 
     relays = [p for top in reversed(bits_of(H)) if top > 1 for p in range(top, H, 2 * top)]
 
-    def x_event(tau, k):
+    def relay(tau, k):
         for piece in relays:
             got_piece(tau, piece, k)
-            forward(tau, piece, k)
-
-    order = list(range(E - 1, 0, -1))
+            for build in forwards(tau, piece, k):
+                build().start()
+
+    def x_event(tau, n):
+        if n == 0:
+            relay(tau, 0)
+        else:
+            by_class(lambda kind: relay(tau, arrivals[kind][n - 1]))
 
     def gather_events(tau):
         events = [functools.partial(x_event, tau, 0)]
-        for k in order:
-            events.insert(-1, functools.partial(z_event, tau, k))
-            events.append(functools.partial(x_event, tau, k))
+        for n in range(E - 1):
+            events.insert(-1, functools.partial(z_event, tau, n))
+            events.append(functools.partial(x_event, tau, n + 1))
         return events
 
     def complete(tau):
@@ -247,7 +284,9 @@
 
     stat_copies = all_to_hid(stat_send, stat_recv, s_send, s_recv)
 
-    dispatch(COT, 0, cot_ref[...], True)
+    dispatch(COT, 0, cot_ref[...])
+    first_wave(COT)
+    forward(COT, 0)
 
     total = stats.T[0:32]
     for m, copy in enumerate(stat_copies):
@@ -270,8 +309,8 @@
         put(keep + 3, first_score - second_score)
         return (ref[...].astype(F32) * scale * gain).astype(BF16)
 
-    dispatch(NXT, 2, finish_norm(16, 2, next_ref, 4), False)
-    dispatch(SAV, 0, finish_norm(0, 0, saved_ref, 0), False)
+    dispatch(NXT, 2, finish_norm(16, 2, next_ref, 4))
+    dispatch(SAV, 0, finish_norm(0, 0, saved_ref, 0))
 
     far = [(cot_ref, far_cot), (saved_ref, far_saved), (gain_ref, far_gain), (table_ref, far_table), (cols, far_cols)]
 
@@ -288,8 +327,7 @@
         for n in range(len(far)):
             far_copy(n).start()
 
-    def reduce_step(which, acc, i):
-        m_now, c = place_of(i)
+    def reduce_step(which, acc, m_now, c):
 
         @pl.when(m_now == 0)
         def _():
@@ -386,12 +424,12 @@
 
     for event in gather_events(COT):
         event()
-    forward(NXT, 0, 0)
     complete(COT)
     next_events = gather_events(NXT)
-    early = 4 if E == 4 else len(next_events) // 2
-    spots = [(1 + 5 * n // early) for n in range(early)]
-    gh_events = place(next_events[:early], spots, n_tiles)
+    for event in next_events[:2]:
+        event()
+    early = len(next_events) // 2 + 1
+    gh_events = place(next_events[2:early], [n_tiles // 2 + n for n in range(early - 2)], n_tiles)
 
     @pl.loop(0, n_tiles)
     def _(j):
@@ -410,14 +448,14 @@
 
     for event in next_events[early:]:
         event()
-    forward(SAV, 0, 0)
     complete(NXT)
 
     saved_events = gather_events(SAV)
-    late = 1
+    saved_events[0]()
+    late = 2
     count = len(saved_events) - late
-    spots = [(n_tiles - 1) * n // max(1, count - 1) for n in range(count)]
-    up_events = place(saved_events[:count], spots, n_tiles)
+    spots = [n_tiles - count + n for n in range(count)]
+    up_events = place(saved_events[1:count], [max(0, spot) for spot in spots[1:]], n_tiles)
 
     @pl.loop(0, n_tiles)
     def _(j):
@@ -425,21 +463,23 @@
         slot = lax.rem(j, A_SLOTS)
         for copy in a_copies("pair", j, slot):
             copy.wait()
-        gate = dot(rows[NXT], wa[slot, 0, :, 0:tn])
-        up = dot(rows[NXT], wa[slot, 1, :, 0:tn])
+        both = dot(rows[NXT], wa[slot, :, 0:2 * tn])
+        gate, up = both[:, 0:tn], both[:, tn:2 * tn]
         hid_n[:, pl.ds(pl.multiple_of(j * tn, tn), tn)] = (gate * jax.nn.sigmoid(gate) * up).astype(BF16)
         run(up_events, j)
 
-    out_events = place(saved_events[count:], [(3 * out_items) // 4] * late, out_items)
+    out_events = place(saved_events[count:], [out_items // 4, out_items // 2], out_items)
 
     @pl.loop(0, out_items)
     def _(i):
         g = n_tiles + i
         start_a(g + A_SLOTS - 1)
         slot = lax.rem(g, A_SLOTS)
-        for half, copy in enumerate(a_copies("out", i, slot)):
-            copy.wait()
-            reduce_step(0, dot(hid_n[...], wa[slot, half, 0:ffd, 0:tw]), 2 * i + half)
+        out_copy(i, slot).wait()
+        acc = dot(hid_n[...], wa[slot, 0:ffd, 0:2 * tw])
+        m, c = place_of(i, "out")
+        for half in range(2):
+            reduce_step(0, acc[:, half * tw:(half + 1) * tw], m, 2 * c + half)
         run(out_events, i)
 
     complete(SAV)
@@ -456,8 +496,8 @@
         slot = lax.rem(g, A_SLOTS)
         for copy in a_copies("pair", j, slot):
             copy.wait()
-        gate = dot(rows[SAV], wa[slot, 0, :, 0:tn])
-        up = dot(rows[SAV], wa[slot, 1, :, 0:tn])
+        both = dot(rows[SAV], wa[slot, :, 0:2 * tn])
+        gate, up = both[:, 0:tn], both[:, tn:2 * tn]
         part = pl.ds(pl.multiple_of(j * tn, tn), tn)
         grad = gh[:, part]
         sig = jax.nn.sigmoid(gate)
@@ -493,9 +533,8 @@
         dots_acc[0:T, 0:1] = gap
 
     late_events = [(1 + 2 * n, functools.partial(home_event, 0, c)) for n, c in enumerate(c for c in range(n_cols) if c not in in_gate)]
-    soon = [c for c in range(n_cols) if H * (c + 2) - 1 < steps]
-    back_events = late_events + [(H * (c + 2) - 1, functools.partial(home_event, 1, c)) for c in soon]
-    back_events += [((steps * 5) // 8, dots_event), ((steps * 3) // 4, forward_out)]
+    soon = [c for c in range(n_cols) if H * (c + 2) < steps]
+    back_events = late_events + [(H * (c + 2), functools.partial(home_event, 1, c)) for c in soon]
 
     @pl.loop(0, steps)
     def _(i):
@@ -508,12 +547,15 @@
             copy.wait()
         slot = lax.rem(i, R_SLOTS)
         acc = dot(grads[0], wr[slot, 0:tw, 0:ffd], NT) + dot(grads[1], wr[slot, 0:tw, ffd:2 * ffd], NT)
-        reduce_step(1, acc, i)
+        reduce_step(1, acc, *place_of(i, "back"))
         run(back_events, i)
 
-    for c in range(n_cols):
-        if c not in soon:
-            home_event(1, c)
+    later = [c for c in range(n_cols) if c not in soon]
+    for c in later[:-1]:
+        home_event(1, c)
+    forward_out()
+    dots_event()
+    home_event(1, later[-1])
     picks = selectors(0)
     inner = jnp.zeros((T, 1), F32)
     for c in range(n_cols):
@@ -594,6 +636,13 @@
 
     for build in to_send:
         build().wait_send()
+    for tau in range(3):
+        for k in range(E):
+            if k:
+                dispatch_copy(tau, k).wait_send()
+            for piece in [0] + relays:
+                for build in forwards(tau, piece, k):
+                    build().wait_send()
     for which in range(2):
         for m in range(1, H):
             for c in range(n_cols):
@@ -626,7 +675,7 @@
     scratch = [
         pltpu.VMEM((3, all_rows, D), BF16),
         pltpu.VMEM((3, E - 1, cap, F), BF16),
-        pltpu.VMEM((A_SLOTS, 2, D, deep), BF16),
+        pltpu.VMEM((A_SLOTS, D, 2 * deep), BF16),
         pltpu.VMEM((R_SLOTS, deep, wide), BF16),
         pltpu.VMEM((all_rows, ffd), F32),
         pltpu.VMEM((all_rows, ffd), BF16),

time: 149 us -> 131 us (0.88)
  Pallas kernels: 147 us -> 128 us
    pallas_call x1, Pallas kernels: 147 us -> 128 us  [per_device(): pl.pallas_call(functools.partial(kernel, (E, H, T, F, D, ffd, cap, tn, tw...]
where the time goes in v2:
time: 131 us; the launch traced here: 130 us
  Pallas kernels  128 us (98%)
  local copies, waits for them, and re-layouts  1.85 us (1%)
    pallas_call x1, Pallas kernels, per_device(): pl.pallas_call(functools.partial(kernel, (E, H, T, F, D, ffd, cap, tn, tw...  128 us

profile of v2, /device:TPU:0, one launch (start us, length us, event | category | flops | bytes accessed | tf_op | source)
XLA Modules:
  0.0 130.4 jit_solution(13035954153174983591)
XLA Ops:
  0.6 127.9 %relay.1 = bf16[2,128,1024]{2,1,0:T(8,128)(2,1)} custom-call(bf16[128,1024]{1,0:T(8,128)(2,1)} %bitcast.18, bf16[128,1024]{1,0:T(8,128)(2,1)} %bitcast.19, bf16[128,1024]{1,0:T(8,128)(2,1)} %bitcast.20, s32[2,128]{1,0:T(2,128)} %bitcast.22, s32[2,128]{1,0:T(2,128)} %bitcast.23, f32[1,1024]{1,0:T(1,128)} %gain_ref.1, f32[4,1024]{1,0:T(4,128)} %bitcast.21, ...), custom_call_target="tpu_custom_call" | custom-call | tf_op jit(solution)/shard_map/relay/pallas_call | solution.py:729
  128.6 1.9 %fusion = (bf16[1,128,1024]{2,1,0:T(8,128)(2,1)}, bf16[1,128,1024]{2,1,0:T(8,128)(2,1)}) fusion(bf16[2,128,1024]{2,1,0:T(8,128)(2,1)} %relay.1), kind=kLoop, calls=%fused_computation | loop fusion | bytes 1048576 | tf_op jit(solution)/shard_map/slice | solution.py:743

commit v3 on v2

--- a/solution.py
+++ b/solution.py
@@ -16,7 +16,7 @@
 LANES = 128
 A_SLOTS = 3
 R_SLOTS = 4
-COT, NXT, SAV = 0, 1, 2
+NXT, SAV, COT = 0, 1, 2
 
 
 def bits_of(count):
@@ -48,7 +48,7 @@
     sizes,
     saved_ref, cot_ref, next_ref, pair_saved_ref, pair_next_ref, gain_ref, table_ref, wg_ref, wu_ref, wd_ref,
     out_ref,
-    rows, slots, wa, wr, gh, hid_n, grads, rs_send, rs_recv, own_part, home_send, home,
+    rows, slots, wa, wr, pair, hid_n, grads, rs_send, rs_recv, own_part, home_send, home,
     stat_send, stat_recv, dots_acc, dots_send, dots_recv, tail_send, tail_recv,
     cols, mixed, there_send, there_recv, far_cot, far_saved, far_value, far_gain, far_table, far_cols, far_tail,
     wa_sem, wr_sem,
@@ -119,7 +119,7 @@
             wr_sem.at[slot, 0])
 
     def back_copies(i):
-        slot = lax.rem(i, R_SLOTS)
+        slot = lax.rem(n_tiles + i, R_SLOTS)
         m, c = place_of(i, "back")
         row = pl.multiple_of(flip(hi, m, H) * F + c * tw, tw)
         return [
@@ -127,6 +127,16 @@
                 w.at[pl.ds(row, tw), :], wr.at[slot, pl.ds(0, tw), pl.ds(half * ffd, ffd)], wr_sem.at[slot, half])
             for half, w in enumerate((wg_ref, wu_ref))
         ]
+
+    def start_r(g):
+        @pl.when(g < n_tiles)
+        def _():
+            gh_copy(g).start()
+
+        @pl.when((g >= n_tiles) & (g < n_tiles + steps))
+        def _():
+            for copy in back_copies(g - n_tiles):
+                copy.start()
 
     for j in range(min(R_SLOTS - 1, n_tiles)):
         gh_copy(none + j).start()
@@ -176,9 +186,8 @@
 
     order = list(range(E - 1, 0, -1))
     inner = flip(lax.rem(me, 2), lax.rem(lax.div(me, 2), 2), 2)
-    first_sends = ([1, 3, 2], [1, 3, 2]) if E == 4 else (order, order)
-    late_send = None
-    arrivals = ([1, 3, 2], [1, 3, 2]) if E == 4 else (order, order)
+    arrivals = [1, 3, 2] if E == 4 else order
+    early_sends = []
 
     def by_class(build):
         if E != 4:
@@ -188,8 +197,9 @@
             pl.when(inner == kind)(functools.partial(build, kind))
 
     def first_wave(tau):
-        by_class(lambda kind: [dispatch_copy(tau, k).start() for k in first_sends[kind]] and None)
-
+        for k in arrivals:
+            if tau != COT or k not in early_sends:
+                dispatch_copy(tau, k).start()
 
     def region(tau, expert, feature):
         return rows.at[tau, pl.ds(pl.multiple_of(expert * cap, 16), cap), pl.ds(pl.multiple_of(feature * F, LANES), F)]
@@ -225,21 +235,16 @@
                 slots[tau, k - 1] = picked
 
     def z_event(tau, n):
-        def take(kind):
-            k = arrivals[kind][n]
-            part = region(tau, exp_peer[k], hi)
-            remote(part, part, z_send.at[tau, k], z_recv.at[tau, k], e=exp_peer[k]).wait_recv()
-            for build in forwards(tau, 0, k):
-                build().start()
-            if n == 0 and kind == 1 and late_send:
-                dispatch_copy(tau, late_send).start()
-            if tau < SAV and n == E - 2:
-                for k in first_sends[kind]:
-                    dispatch_copy(tau + 1, k).start()
-
-        by_class(take)
-        if tau < SAV and n == 0:
-            forward(tau + 1, 0)
+        k = arrivals[n]
+        part = region(tau, exp_peer[k], hi)
+        remote(part, part, z_send.at[tau, k], z_recv.at[tau, k], e=exp_peer[k]).wait_recv()
+        forward(tau, k)
+        if tau == NXT and n == E - 2:
+            first_wave(SAV)
+        if tau == SAV and n >= E - 3:
+            by_class(lambda kind: first_wave(COT) if kind == E - 2 - n or E != 4 and n == E - 2 else None)
+        if tau + 1 == SAV and n == 0:
+            forward(SAV, 0)
 
     relays = [p for top in reversed(bits_of(H)) if top > 1 for p in range(top, H, 2 * top)]
 
@@ -250,10 +255,7 @@
                 build().start()
 
     def x_event(tau, n):
-        if n == 0:
-            relay(tau, 0)
-        else:
-            by_class(lambda kind: relay(tau, arrivals[kind][n - 1]))
+        relay(tau, arrivals[n - 1] if n else 0)
 
     def gather_events(tau):
         events = [functools.partial(x_event, tau, 0)]
@@ -285,8 +287,9 @@
     stat_copies = all_to_hid(stat_send, stat_recv, s_send, s_recv)
 
     dispatch(COT, 0, cot_ref[...])
-    first_wave(COT)
     forward(COT, 0)
+    for k in early_sends:
+        dispatch_copy(COT, k).start()
 
     total = stats.T[0:32]
     for m, copy in enumerate(stat_copies):
@@ -310,6 +313,8 @@
         return (ref[...].astype(F32) * scale * gain).astype(BF16)
 
     dispatch(NXT, 2, finish_norm(16, 2, next_ref, 4))
+    first_wave(NXT)
+    forward(NXT, 0)
     dispatch(SAV, 0, finish_norm(0, 0, saved_ref, 0))
 
     far = [(cot_ref, far_cot), (saved_ref, far_saved), (gain_ref, far_gain), (table_ref, far_table), (cols, far_cols)]
@@ -341,7 +346,8 @@
                     received(which, m + bit, c)
                     value = value + rs_recv[which, m + bit - 1, c].astype(F32)
                 rs_send[which, m - 1, c] = value.astype(BF16)
-                reduce_copy(which, m, c).start()
+                if which == 1 or m == 1 or m != low_bit(m):
+                    reduce_copy(which, m, c).start()
 
     def reduce_copy(which, m, c):
         return remote(
@@ -419,87 +425,97 @@
         for at, event in events:
             pl.when(index == at)(event)
 
-    def place(events, spots, limit):
-        return [(min(spot, limit - 1), event) for event, spot in zip(events, spots)]
-
-    for event in gather_events(COT):
+    next_events, cot_events = gather_events(NXT), gather_events(COT)
+    for event in next_events[:-2]:
         event()
-    complete(COT)
-    next_events = gather_events(NXT)
-    for event in next_events[:2]:
-        event()
-    early = len(next_events) // 2 + 1
-    gh_events = place(next_events[2:early], [n_tiles // 2 + n for n in range(early - 2)], n_tiles)
-
-    @pl.loop(0, n_tiles)
-    def _(j):
-        @pl.when(j + R_SLOTS - 1 < n_tiles)
-        def _():
-            gh_copy(j + R_SLOTS - 1).start()
-
-        gh_copy(j).wait()
-        slot = lax.rem(j, R_SLOTS)
-        gh[:, pl.ds(pl.multiple_of(j * tn, tn), tn)] = dot(rows[COT], wr[slot, 0:tn, 0:D], NT)
-        run(gh_events, j)
-
-    for i in range(R_SLOTS - 1):
-        for copy in back_copies(none + i):
-            copy.start()
-
-    for event in next_events[early:]:
+    if early_sends:
+        cot_events[0]()
+    for event in next_events[-2:]:
         event()
     complete(NXT)
 
+    def at(events, spots):
+        return list(zip(spots, events))
+
+    def split(event, late, soon):
+        return [(late + (soon - late) * (1 - inner), event)]
+
+    wide_sends = [(m, c) for m in reversed(bits_of(H)) if m > 1 for c in range(n_cols)]
+
+    def wave(start, stop):
+        return [functools.partial(lambda m, c: reduce_copy(0, m, c).start(), m, c) for m, c in wide_sends[start:stop]]
+
+    downs = [functools.partial(home_event, 0, c) for c in range(n_cols)]
+    tuned = E == 4 and H == 4 and n_cols == 4 and n_tiles == 7
     saved_events = gather_events(SAV)
-    saved_events[0]()
-    late = 2
-    count = len(saved_events) - late
-    spots = [n_tiles - count + n for n in range(count)]
-    up_events = place(saved_events[1:count], [max(0, spot) for spot in spots[1:]], n_tiles)
+    if tuned:
+        up_events = at(saved_events[:6], [0, 1, 3, 3, 5, 6])
+        out_events = at(saved_events[6:], [2]) + at(cot_events[:1], [3]) + at(wave(0, 1), [4])
+        gate_events = at(cot_events[2:3], [0]) + at(cot_events[4:5], [3]) + at(wave(1, 4), [3, 3, 3])
+        gate_events += at(cot_events[3:4], [3]) + at(downs[:1], [4]) + at(cot_events[5:], [5, 6])
+        gh_events = at(downs[1:2], [4])
+        back_events = at(downs[2:], [1, 4])
+    else:
+        up_events = at(saved_events, [n_tiles * n // len(saved_events) for n in range(len(saved_events))])
+        out_events = []
+        late_events = cot_events[:1] + cot_events[2:]
+        gate_events = at(late_events, [n_tiles * n // len(late_events) for n in range(len(late_events))])
+        waves = wave(0, len(wide_sends))
+        gate_events += at(waves, [n_tiles - 1] * len(waves))
+        gh_events = []
+        back_events = at(downs, [2 + c for c in range(n_cols)])
+    cot_events[1]()
 
     @pl.loop(0, n_tiles)
     def _(j):
         start_a(j + A_SLOTS - 1)
+        run(up_events, j)
         slot = lax.rem(j, A_SLOTS)
         for copy in a_copies("pair", j, slot):
             copy.wait()
         both = dot(rows[NXT], wa[slot, :, 0:2 * tn])
         gate, up = both[:, 0:tn], both[:, tn:2 * tn]
         hid_n[:, pl.ds(pl.multiple_of(j * tn, tn), tn)] = (gate * jax.nn.sigmoid(gate) * up).astype(BF16)
-        run(up_events, j)
-
-    out_events = place(saved_events[count:], [out_items // 4, out_items // 2], out_items)
 
     @pl.loop(0, out_items)
     def _(i):
         g = n_tiles + i
         start_a(g + A_SLOTS - 1)
+        run(out_events, i)
         slot = lax.rem(g, A_SLOTS)
         out_copy(i, slot).wait()
         acc = dot(hid_n[...], wa[slot, 0:ffd, 0:2 * tw])
         m, c = place_of(i, "out")
         for half in range(2):
             reduce_step(0, acc[:, half * tw:(half + 1) * tw], m, 2 * c + half)
-        run(out_events, i)
 
     complete(SAV)
 
     dots_acc[...] = jnp.zeros_like(dots_acc)
-    down_spots = [1 + 2 * c for c in range(n_cols)]
-    in_gate = [c for c in range(n_cols) if down_spots[c] < n_tiles - 1]
-    gate_events = [(down_spots[c], functools.partial(home_event, 0, c)) for c in in_gate]
-
     @pl.loop(0, n_tiles)
     def _(j):
         g = n_tiles + out_items + j
         start_a(g + A_SLOTS - 1)
+        run(gate_events, j)
         slot = lax.rem(g, A_SLOTS)
         for copy in a_copies("pair", j, slot):
             copy.wait()
+        part = pl.ds(pl.multiple_of(j * tn, tn), tn)
         both = dot(rows[SAV], wa[slot, :, 0:2 * tn])
-        gate, up = both[:, 0:tn], both[:, tn:2 * tn]
+        pair[0, :, part] = both[:, 0:tn]
+        pair[1, :, part] = both[:, tn:2 * tn]
+
+    complete(COT)
+
+    @pl.loop(0, n_tiles)
+    def _(j):
+        start_r(j + R_SLOTS - 1)
+        run(gh_events, j)
+        gh_copy(j).wait()
+        slot = lax.rem(j, R_SLOTS)
+        grad = dot(rows[COT], wr[slot, 0:tn, 0:D], NT)
         part = pl.ds(pl.multiple_of(j * tn, tn), tn)
-        grad = gh[:, part]
+        gate, up = pair[0, :, part], pair[1, :, part]
         sig = jax.nn.sigmoid(gate)
         silu = gate * sig
         hidden = (silu * up).astype(BF16).astype(F32)
@@ -510,7 +526,6 @@
         for n in range(1, tn // LANES):
             partial = partial + product[:, n * LANES:(n + 1) * LANES]
         dots_acc[...] += partial
-        run(gate_events, j)
 
     def dots_copy(k):
         return remote(dots_send, dots_recv.at[k - 1], d_send.at[k], d_recv.at[k], e=exp_peer[k])
@@ -532,23 +547,18 @@
                 gap = gap + sign * jnp.sum(jnp.where(wide_i == spot, row, 0.0), axis=1, keepdims=True)
         dots_acc[0:T, 0:1] = gap
 
-    late_events = [(1 + 2 * n, functools.partial(home_event, 0, c)) for n, c in enumerate(c for c in range(n_cols) if c not in in_gate)]
-    soon = [c for c in range(n_cols) if H * (c + 2) < steps]
-    back_events = late_events + [(H * (c + 2), functools.partial(home_event, 1, c)) for c in soon]
+    soon = [c for c in range(n_cols) if H * (c + 2) + 1 < steps]
+    back_events += [(H * (c + 2) + 1, functools.partial(home_event, 1, c)) for c in soon]
 
     @pl.loop(0, steps)
     def _(i):
-        @pl.when(i + R_SLOTS - 1 < steps)
-        def _():
-            for copy in back_copies(i + R_SLOTS - 1):
-                copy.start()
-
+        start_r(n_tiles + i + R_SLOTS - 1)
+        run(back_events, i)
         for copy in back_copies(i):
             copy.wait()
-        slot = lax.rem(i, R_SLOTS)
+        slot = lax.rem(n_tiles + i, R_SLOTS)
         acc = dot(grads[0], wr[slot, 0:tw, 0:ffd], NT) + dot(grads[1], wr[slot, 0:tw, ffd:2 * ffd], NT)
         reduce_step(1, acc, *place_of(i, "back"))
-        run(back_events, i)
 
     later = [c for c in range(n_cols) if c not in soon]
     for c in later[:-1]:
@@ -677,7 +687,7 @@
         pltpu.VMEM((3, E - 1, cap, F), BF16),
         pltpu.VMEM((A_SLOTS, D, 2 * deep), BF16),
         pltpu.VMEM((R_SLOTS, deep, wide), BF16),
-        pltpu.VMEM((all_rows, ffd), F32),
+        pltpu.VMEM((2, all_rows, ffd), F32),
         pltpu.VMEM((all_rows, ffd), BF16),
         pltpu.VMEM((2, all_rows, ffd), BF16),
         pltpu.VMEM((2, H - 1, n_cols, all_rows, tw), BF16),

time: 131 us -> 124 us (0.947)
  Pallas kernels: 128 us -> 121 us
    pallas_call x1, Pallas kernels: 128 us -> 121 us  [per_device(): pl.pallas_call(functools.partial(kernel, (E, H, T, F, D, ffd, cap, tn, tw...]
where the time goes in v3:
time: 124 us
  Pallas kernels  121 us (98%)
  local copies, waits for them, and re-layouts  1.85 us (1%)
    pallas_call x1, Pallas kernels, per_device(): pl.pallas_call(functools.partial(kernel, (E, H, T, F, D, ffd, cap, tn, tw...  121 us

profile of v3, /device:TPU:0, one launch (start us, length us, event | category | flops | bytes accessed | tf_op | source)
XLA Modules:
  0.0 123.8 jit_solution(9380457307470314158)
XLA Ops:
  0.6 121.3 %relay.1 = bf16[2,128,1024]{2,1,0:T(8,128)(2,1)} custom-call(bf16[128,1024]{1,0:T(8,128)(2,1)} %bitcast.18, bf16[128,1024]{1,0:T(8,128)(2,1)} %bitcast.19, bf16[128,1024]{1,0:T(8,128)(2,1)} %bitcast.20, s32[2,128]{1,0:T(2,128)} %bitcast.22, s32[2,128]{1,0:T(2,128)} %bitcast.23, f32[1,1024]{1,0:T(1,128)} %gain_ref.1, f32[4,1024]{1,0:T(4,128)} %bitcast.21, ...), custom_call_target="tpu_custom_call" | custom-call | tf_op jit(solution)/shard_map/relay/pallas_call | solution.py:739
  121.9 1.9 %fusion = (bf16[1,128,1024]{2,1,0:T(8,128)(2,1)}, bf16[1,128,1024]{2,1,0:T(8,128)(2,1)}) fusion(bf16[2,128,1024]{2,1,0:T(8,128)(2,1)} %relay.1), kind=kLoop, calls=%fused_computation | loop fusion | bytes 1048576 | tf_op jit(solution)/shard_map/slice | solution.py:753

commit v4 on v3

--- a/solution.py
+++ b/solution.py
@@ -50,10 +50,10 @@
     out_ref,
     rows, slots, wa, wr, pair, hid_n, grads, rs_send, rs_recv, own_part, home_send, home,
     stat_send, stat_recv, dots_acc, dots_send, dots_recv, tail_send, tail_recv,
-    cols, mixed, there_send, there_recv, far_cot, far_saved, far_value, far_gain, far_table, far_cols, far_tail,
+    cols, mixed, there_send, there_recv, far_cot, far_saved, far_value, far_gain, far_table, far_cols, far_tail, scale_send, scale_recv, scales,
     wa_sem, wr_sem,
     z_send, z_recv, g_send, g_recv, s_send, s_recv, r_send, r_recv,
-    b_send, b_recv, d_send, d_recv, t_send, t_recv, y_send, y_recv, e_send, e_recv, f_send, f_recv,
+    b_send, b_recv, d_send, d_recv, t_send, t_recv, y_send, y_recv, e_send, e_recv, f_send, f_recv, c_send, c_recv,
 ):
     E, H, T, F, D, ffd, cap, tn, tw = sizes
     n_tiles, n_cols = ffd // tn, F // tw
@@ -174,15 +174,15 @@
     def put(n, value):
         cols[:, n:n + 1] = value
 
+    kept_ranks = []
     for n, base in enumerate((0, 2)):
         hits = jnp.where(lane_f == route_cols[base], 1.0, 0.0) + jnp.where(lane_f == route_cols[base + 1], 1.0, 0.0)
         ranks = dot(lower, hits.astype(BF16))
+        kept_ranks.append((hits, ranks))
         for c in range(2):
             route = route_cols[base + c]
             put(16 + 2 * n + c, jnp.sum(jnp.where(lane_f == route, ranks, 0.0), axis=1, keepdims=True))
             put(20 + 2 * n + c, route)
-
-    pl.semaphore_wait(barrier, len(partners))
 
     order = list(range(E - 1, 0, -1))
     inner = flip(lax.rem(me, 2), lax.rem(lax.div(me, 2), 2), 2)
@@ -243,7 +243,7 @@
             first_wave(SAV)
         if tau == SAV and n >= E - 3:
             by_class(lambda kind: first_wave(COT) if kind == E - 2 - n or E != 4 and n == E - 2 else None)
-        if tau + 1 == SAV and n == 0:
+        if tau + 1 == SAV and n == E - 2:
             forward(SAV, 0)
 
     relays = [p for top in reversed(bits_of(H)) if top > 1 for p in range(top, H, 2 * top)]
@@ -284,20 +284,21 @@
             send(lambda copy=copy: copy)
         return copies
 
+    dispatch(NXT, 2, (next_ref[...].astype(F32) * gain).astype(BF16))
+    dispatch(COT, 0, cot_ref[...])
+
+    pl.semaphore_wait(barrier, len(partners))
     stat_copies = all_to_hid(stat_send, stat_recv, s_send, s_recv)
-
-    dispatch(COT, 0, cot_ref[...])
+    first_wave(NXT)
+    forward(NXT, 0)
     forward(COT, 0)
-    for k in early_sends:
-        dispatch_copy(COT, k).start()
-
     total = stats.T[0:32]
     for m, copy in enumerate(stat_copies):
         copy.wait_recv()
         total = total + stat_recv[m]
     stats = jnp.concatenate([total, jnp.zeros((LANES - 32, T), F32)], axis=0).T
 
-    def finish_norm(offset, base, ref, keep):
+    def finish_norm(offset, base, keep):
         scale = lax.rsqrt(stats[:, offset:offset + 1] / D + EPSILON)
         first_score = jnp.zeros((T, 1), F32)
         second_score = jnp.zeros((T, 1), F32)
@@ -310,12 +311,25 @@
         put(keep + 1, jax.nn.sigmoid(second - first))
         put(keep + 2, scale)
         put(keep + 3, first_score - second_score)
-        return (ref[...].astype(F32) * scale * gain).astype(BF16)
-
-    dispatch(NXT, 2, finish_norm(16, 2, next_ref, 4))
-    first_wave(NXT)
-    forward(NXT, 0)
-    dispatch(SAV, 0, finish_norm(0, 0, saved_ref, 0))
+        return scale
+
+    scale = finish_norm(16, 2, 4)
+    hits, ranks = kept_ranks[1]
+    for k in range(E):
+        named = lane == exp_peer[k]
+        rank = jnp.sum(jnp.where(named, ranks, 0.0), axis=1, keepdims=True)
+        hit = jnp.sum(jnp.where(named, hits, 0.0), axis=1, keepdims=True)
+        rank = jnp.where(hit > 0.5, rank, -1.0)
+        row = jnp.sum(jnp.where(lane_f == rank, scale, 0.0), axis=0, keepdims=True)
+        scale_send[k] = jnp.broadcast_to(row, (8, LANES))
+
+    def scale_copy(k):
+        return remote(scale_send.at[k], scale_recv.at[k - 1], c_send.at[k], c_recv.at[k], e=exp_peer[k])
+
+    for k in range(1, E):
+        send(functools.partial(scale_copy, k))
+    scale = finish_norm(0, 0, 0)
+    dispatch(SAV, 0, (saved_ref[...].astype(F32) * scale * gain).astype(BF16))
 
     far = [(cot_ref, far_cot), (saved_ref, far_saved), (gain_ref, far_gain), (table_ref, far_table), (cols, far_cols)]
 
@@ -371,7 +385,7 @@
             received(which, bit, c)
             value = value + rs_recv[which, bit - 1, c].astype(F32)
         home_send[which, c] = value.astype(BF16)
-        for k in order:
+        for k in arrivals:
             send(functools.partial(home_copy, which, k, c))
         mine = pl.ds(pl.multiple_of(me * cap, 16), cap)
         home[which, mine, c * tw:(c + 1) * tw] = home_send[which, c, mine, :]
@@ -433,6 +447,11 @@
     for event in next_events[-2:]:
         event()
     complete(NXT)
+    for k in range(E):
+        if k:
+            scale_copy(k).wait_recv()
+        row = scale_recv[k - 1, 0:1] if k else scale_send[0, 0:1]
+        scales[pl.ds(pl.multiple_of(exp_peer[k] * cap, 16), cap), :] = jnp.broadcast_to(row, (LANES, LANES)).T[0:cap]
 
     def at(events, spots):
         return list(zip(spots, events))
@@ -449,12 +468,11 @@
     tuned = E == 4 and H == 4 and n_cols == 4 and n_tiles == 7
     saved_events = gather_events(SAV)
     if tuned:
-        up_events = at(saved_events[:6], [0, 1, 3, 3, 5, 6])
-        out_events = at(saved_events[6:], [2]) + at(cot_events[:1], [3]) + at(wave(0, 1), [4])
-        gate_events = at(cot_events[2:3], [0]) + at(cot_events[4:5], [3]) + at(wave(1, 4), [3, 3, 3])
-        gate_events += at(cot_events[3:4], [3]) + at(downs[:1], [4]) + at(cot_events[5:], [5, 6])
-        gh_events = at(downs[1:2], [4])
-        back_events = at(downs[2:], [1, 4])
+        up_events = at(saved_events[:6], [0, 1, 2, 3, 4, 5])
+        out_events = at(saved_events[6:], [1]) + at(cot_events[:1], [1]) + at(wave(0, 1), [3]) + at(cot_events[2:4], [5, 5])
+        gate_events = at(cot_events[4:5], [1]) + at(wave(1, 4), [1, 1, 1]) + at(downs[:1], [2]) + at(cot_events[5:], [3, 5])
+        gh_events = at(downs[1:3], [1, 4])
+        back_events = at(downs[3:], [1])
     else:
         up_events = at(saved_events, [n_tiles * n // len(saved_events) for n in range(len(saved_events))])
         out_events = []
@@ -473,7 +491,7 @@
         slot = lax.rem(j, A_SLOTS)
         for copy in a_copies("pair", j, slot):
             copy.wait()
-        both = dot(rows[NXT], wa[slot, :, 0:2 * tn])
+        both = dot(rows[NXT], wa[slot, :, 0:2 * tn]) * scales[:, 0:1]
         gate, up = both[:, 0:tn], both[:, tn:2 * tn]
         hid_n[:, pl.ds(pl.multiple_of(j * tn, tn), tn)] = (gate * jax.nn.sigmoid(gate) * up).astype(BF16)
 
@@ -713,6 +731,9 @@
         pltpu.VMEM((E, F), F32),
         pltpu.VMEM((T, LANES), F32),
         pltpu.VMEM((H, 8, T), F32),
+        pltpu.VMEM((E, 8, LANES), F32),
+        pltpu.VMEM((E - 1, 8, LANES), F32),
+        pltpu.VMEM((all_rows, LANES), F32),
         dma((A_SLOTS, 2)),
         dma((R_SLOTS, 2)),
         dma((3, E)),
@@ -735,6 +756,8 @@
         dma((5 + n_cols,)),
         dma((H,)),
         dma((H,)),
+        dma((E,)),
+        dma((E,)),
     ]
     result = pl.pallas_call(
         functools.partial(kernel, (E, H, T, F, D, ffd, cap, tn, tw)),

time: 124 us -> 121 us (0.976)
  Pallas kernels: 121 us -> 119 us
    pallas_call x1, Pallas kernels: 121 us -> 119 us  [per_device(): pl.pallas_call(functools.partial(kernel, (E, H, T, F, D, ffd, cap, tn, tw...]
where the time goes in v4:
time: 121 us
  Pallas kernels  119 us (98%)
  local copies, waits for them, and re-layouts  1.85 us (2%)
    pallas_call x1, Pallas kernels, per_device(): pl.pallas_call(functools.partial(kernel, (E, H, T, F, D, ffd, cap, tn, tw...  119 us

profile of v4, /device:TPU:0, one launch (start us, length us, event | category | flops | bytes accessed | tf_op | source)
XLA Modules:
  0.0 121.0 jit_solution(8332774325984276427)
XLA Ops:
  0.6 118.5 %relay.1 = bf16[2,128,1024]{2,1,0:T(8,128)(2,1)} custom-call(bf16[128,1024]{1,0:T(8,128)(2,1)} %bitcast.18, bf16[128,1024]{1,0:T(8,128)(2,1)} %bitcast.19, bf16[128,1024]{1,0:T(8,128)(2,1)} %bitcast.20, s32[2,128]{1,0:T(2,128)} %bitcast.22, s32[2,128]{1,0:T(2,128)} %bitcast.23, f32[1,1024]{1,0:T(1,128)} %gain_ref.1, f32[4,1024]{1,0:T(4,128)} %bitcast.21, ...), custom_call_target="tpu_custom_call" | custom-call | tf_op jit(solution)/shard_map/relay/pallas_call | solution.py:762
  119.2 1.9 %fusion = (bf16[1,128,1024]{2,1,0:T(8,128)(2,1)}, bf16[1,128,1024]{2,1,0:T(8,128)(2,1)}) fusion(bf16[2,128,1024]{2,1,0:T(8,128)(2,1)} %relay.1), kind=kLoop, calls=%fused_computation | loop fusion | bytes 1048576 | tf_op jit(solution)/shard_map/slice | solution.py:776

commit v5 on v4

--- a/solution.py
+++ b/solution.py
@@ -50,14 +50,14 @@
     out_ref,
     rows, slots, wa, wr, pair, hid_n, grads, rs_send, rs_recv, own_part, home_send, home,
     stat_send, stat_recv, dots_acc, dots_send, dots_recv, tail_send, tail_recv,
-    cols, mixed, there_send, there_recv, far_cot, far_saved, far_value, far_gain, far_table, far_cols, far_tail, scale_send, scale_recv, scales,
+    cols, mixed, there_send, there_recv, far_cot, far_saved, far_value, far_gain, far_table, far_cols, far_tail, scale_send, scale_recv, scales, leans,
     wa_sem, wr_sem,
     z_send, z_recv, g_send, g_recv, s_send, s_recv, r_send, r_recv,
     b_send, b_recv, d_send, d_recv, t_send, t_recv, y_send, y_recv, e_send, e_recv, f_send, f_recv, c_send, c_recv,
 ):
-    E, H, T, F, D, ffd, cap, tn, tw = sizes
-    n_tiles, n_cols = ffd // tn, F // tw
-    steps = H * n_cols
+    E, H, T, F, D, ffd, cap, tn, tw, tc = sizes
+    n_tiles, n_wide, n_cols = ffd // tn, F // tw, F // tc
+    steps = H * n_wide
     all_rows = E * cap
     sec, me, hi = lax.axis_index("section"), lax.axis_index("expert"), lax.axis_index("hid")
     hid_peer = [flip(hi, m, H) for m in range(H)]
@@ -76,11 +76,16 @@
         build().start()
         to_send.append(build)
 
+    back_order = [(m, c) for c in range(n_wide) for m in reversed(range(H))]
+    if H == 4 and n_wide == 4:
+        back_order = [(m, c) for c in (0, 1) for m in (3, 2)] + [(1, 0), (0, 0)]
+        back_order += [(m, c) for c in (2, 3) for m in (3, 2)] + [(m, c) for c in (1, 2, 3) for m in (1, 0)]
+
     def place_of(i, kind):
         if kind == "out":
-            return H - 1 - lax.div(i, n_cols // 2), lax.rem(i, n_cols // 2)
-        at = lax.rem(i, H)
-        return H - 1 - 2 * at + lax.div(at, H // 2) * (H - 1), lax.div(i, H)
+            return H - 1 - lax.div(i, n_wide // 2), lax.rem(i, n_wide // 2)
+        code = sum(jnp.where(i == j, m * n_wide + c, 0) for j, (m, c) in enumerate(back_order))
+        return lax.div(code, n_wide), lax.rem(code, n_wide)
 
     def out_copy(i, slot):
         m, c = place_of(i, "out")
@@ -187,7 +192,6 @@
     order = list(range(E - 1, 0, -1))
     inner = flip(lax.rem(me, 2), lax.rem(lax.div(me, 2), 2), 2)
     arrivals = [1, 3, 2] if E == 4 else order
-    early_sends = []
 
     def by_class(build):
         if E != 4:
@@ -198,8 +202,7 @@
 
     def first_wave(tau):
         for k in arrivals:
-            if tau != COT or k not in early_sends:
-                dispatch_copy(tau, k).start()
+            dispatch_copy(tau, k).start()
 
     def region(tau, expert, feature):
         return rows.at[tau, pl.ds(pl.multiple_of(expert * cap, 16), cap), pl.ds(pl.multiple_of(feature * F, LANES), F)]
@@ -331,13 +334,13 @@
     scale = finish_norm(0, 0, 0)
     dispatch(SAV, 0, (saved_ref[...].astype(F32) * scale * gain).astype(BF16))
 
-    far = [(cot_ref, far_cot), (saved_ref, far_saved), (gain_ref, far_gain), (table_ref, far_table), (cols, far_cols)]
+    far = [(cols, far_cols), (gain_ref, far_gain), (table_ref, far_table), (cot_ref, far_cot), (saved_ref, far_saved)]
 
     def far_copy(n):
         return remote(far[n][0], far[n][1], e_send.at[n], e_recv.at[n], s=1 - sec)
 
     def far_value_copy(c):
-        part = pl.ds(c * tw, tw)
+        part = pl.ds(c * tc, tc)
         n = len(far) + c
         return remote(there_send.at[:, part], far_value.at[:, part], e_send.at[n], e_recv.at[n], s=1 - sec)
 
@@ -346,22 +349,31 @@
         for n in range(len(far)):
             far_copy(n).start()
 
-    def reduce_step(which, acc, m_now, c):
-
+    def lean_of(place_in, kept, table, gains):
+        total = jnp.zeros((T, F), F32)
+        for e in range(E):
+            sign = jnp.where(kept[:, 20:21] == e, 1.0, 0.0) - jnp.where(kept[:, 21:22] == e, 1.0, 0.0)
+            total = total + sign * table[e:e + 1, :]
+        leans[place_in] = kept[:, 2:3] * total * gains[...]
+
+    def reduce_step(which, acc, m_now, first, count):
         @pl.when(m_now == 0)
         def _():
-            own_part[which, c] = acc
+            for n in range(count):
+                own_part[which, first + n] = acc[:, n * tc:(n + 1) * tc]
 
         for m in range(1, H):
             @pl.when(m_now == m)
             def _():
-                value = acc
-                for bit in bits_of(low_bit(m) * 2)[:-1]:
-                    received(which, m + bit, c)
-                    value = value + rs_recv[which, m + bit - 1, c].astype(F32)
-                rs_send[which, m - 1, c] = value.astype(BF16)
-                if which == 1 or m == 1 or m != low_bit(m):
-                    reduce_copy(which, m, c).start()
+                for n in range(count):
+                    c = first + n
+                    value = acc[:, n * tc:(n + 1) * tc]
+                    for bit in bits_of(low_bit(m) * 2)[:-1]:
+                        received(which, m + bit, c)
+                        value = value + rs_recv[which, m + bit - 1, c].astype(F32)
+                    rs_send[which, m - 1, c] = value.astype(BF16)
+                    if which == 1 or m == 1 or m != low_bit(m):
+                        reduce_copy(which, m, c).start()
 
     def reduce_copy(which, m, c):
         return remote(
@@ -372,7 +384,7 @@
         reduce_copy(which, m, c).wait_recv()
 
     def home_region(which, expert, c):
-        return home.at[which, pl.ds(pl.multiple_of(expert * cap, 16), cap), pl.ds(c * tw, tw)]
+        return home.at[which, pl.ds(pl.multiple_of(expert * cap, 16), cap), pl.ds(c * tc, tc)]
 
     def home_copy(which, k, c):
         return remote(
@@ -388,7 +400,7 @@
         for k in arrivals:
             send(functools.partial(home_copy, which, k, c))
         mine = pl.ds(pl.multiple_of(me * cap, 16), cap)
-        home[which, mine, c * tw:(c + 1) * tw] = home_send[which, c, mine, :]
+        home[which, mine, c * tc:(c + 1) * tc] = home_send[which, c, mine, :]
 
     def home_wait(which, c):
         for k in order:
@@ -404,8 +416,8 @@
             picks.append(jnp.where(wide_i == route * cap + rank, 1.0, 0.0).astype(BF16))
         return picks
 
-    def blended(which, n, keep, c, picks):
-        part = home[which, :, c * tw:(c + 1) * tw]
+    def blended(which, keep, part, picks):
+        part = home[which, :, part]
         return cols[:, keep:keep + 1] * dot(picks[0], part) + cols[:, keep + 1:keep + 2] * dot(picks[1], part)
 
     def there_copy(n, height):
@@ -417,10 +429,11 @@
 
     def forward_out():
         picks = selectors(1)
-        for c in range(n_cols):
-            home_wait(0, c)
+        for c in range(n_wide):
+            for n in range(c * tw // tc, (c + 1) * tw // tc):
+                home_wait(0, n)
             part = slice(c * tw, (c + 1) * tw)
-            value = (next_ref[:, part].astype(F32) + blended(0, 1, 4, c, picks)).astype(BF16)
+            value = (next_ref[:, part].astype(F32) + blended(0, 4, part, picks)).astype(BF16)
 
             @pl.when(sec == 0)
             def _():
@@ -442,8 +455,14 @@
     next_events, cot_events = gather_events(NXT), gather_events(COT)
     for event in next_events[:-2]:
         event()
-    if early_sends:
-        cot_events[0]()
+    lean_of(0, cols, table_ref, gain_ref)
+
+    @pl.when(sec == 0)
+    def _():
+        for n in range(len(far)):
+            far_copy(n).wait_recv()
+        lean_of(1, far_cols, far_table, far_gain)
+
     for event in next_events[-2:]:
         event()
     complete(NXT)
@@ -465,14 +484,15 @@
         return [functools.partial(lambda m, c: reduce_copy(0, m, c).start(), m, c) for m, c in wide_sends[start:stop]]
 
     downs = [functools.partial(home_event, 0, c) for c in range(n_cols)]
-    tuned = E == 4 and H == 4 and n_cols == 4 and n_tiles == 7
+    tuned = E == 4 and H == 4 and n_cols == 8 and n_wide == 4 and n_tiles == 7
     saved_events = gather_events(SAV)
     if tuned:
         up_events = at(saved_events[:6], [0, 1, 2, 3, 4, 5])
-        out_events = at(saved_events[6:], [1]) + at(cot_events[:1], [1]) + at(wave(0, 1), [3]) + at(cot_events[2:4], [5, 5])
-        gate_events = at(cot_events[4:5], [1]) + at(wave(1, 4), [1, 1, 1]) + at(downs[:1], [2]) + at(cot_events[5:], [3, 5])
-        gh_events = at(downs[1:3], [1, 4])
-        back_events = at(downs[3:], [1])
+        out_events = at(saved_events[6:], [1]) + at(cot_events[:1], [2]) + at(cot_events[2:3], [6])
+        gate_events = at(cot_events[3:5], [1, 1]) + at(wave(0, 8), [1] * 8) + at(cot_events[5:], [4, 6])
+        gh_events = at(downs[:4], [1, 1, 4, 5])
+        back_events = at(downs[4:], [1, 1, 4, 5])
+        back_spots = [6, 8, 12, 12, 14]
     else:
         up_events = at(saved_events, [n_tiles * n // len(saved_events) for n in range(len(saved_events))])
         out_events = []
@@ -482,6 +502,7 @@
         gate_events += at(waves, [n_tiles - 1] * len(waves))
         gh_events = []
         back_events = at(downs, [2 + c for c in range(n_cols)])
+        back_spots = []
     cot_events[1]()
 
     @pl.loop(0, n_tiles)
@@ -504,8 +525,7 @@
         out_copy(i, slot).wait()
         acc = dot(hid_n[...], wa[slot, 0:ffd, 0:2 * tw])
         m, c = place_of(i, "out")
-        for half in range(2):
-            reduce_step(0, acc[:, half * tw:(half + 1) * tw], m, 2 * c + half)
+        reduce_step(0, acc, m, c * (2 * tw // tc), 2 * tw // tc)
 
     complete(SAV)
 
@@ -565,8 +585,7 @@
                 gap = gap + sign * jnp.sum(jnp.where(wide_i == spot, row, 0.0), axis=1, keepdims=True)
         dots_acc[0:T, 0:1] = gap
 
-    soon = [c for c in range(n_cols) if H * (c + 2) + 1 < steps]
-    back_events += [(H * (c + 2) + 1, functools.partial(home_event, 1, c)) for c in soon]
+    back_events += at([functools.partial(home_event, 1, c) for c in range(n_cols)], back_spots)
 
     @pl.loop(0, steps)
     def _(i):
@@ -576,21 +595,23 @@
             copy.wait()
         slot = lax.rem(n_tiles + i, R_SLOTS)
         acc = dot(grads[0], wr[slot, 0:tw, 0:ffd], NT) + dot(grads[1], wr[slot, 0:tw, ffd:2 * ffd], NT)
-        reduce_step(1, acc, *place_of(i, "back"))
-
-    later = [c for c in range(n_cols) if c not in soon]
-    for c in later[:-1]:
+        m, c = place_of(i, "back")
+        reduce_step(1, acc, m, c * (tw // tc), tw // tc)
+
+    later = list(range(len(back_spots), n_cols))
+    for c in later[:1]:
         home_event(1, c)
     forward_out()
     dots_event()
-    home_event(1, later[-1])
+    for c in later[1:]:
+        home_event(1, c)
     picks = selectors(0)
     inner = jnp.zeros((T, 1), F32)
     for c in range(n_cols):
         home_wait(1, c)
-        part = slice(c * tw, (c + 1) * tw)
-        value = blended(1, 0, 0, c, picks) * gain_ref[:, part]
-        mixed[:, part] = value
+        part = slice(c * tc, (c + 1) * tc)
+        value = blended(1, 0, part, picks) * gain_ref[:, part]
+        mixed[:, part] = cot_ref[:, part].astype(F32) + cols[:, 2:3] * value
 
         @pl.when(sec == 1)
         def _():
@@ -608,22 +629,13 @@
     def far_tail_copy(m):
         return remote(tail_send, far_tail.at[m], f_send.at[m], f_recv.at[m], h=hid_peer[m], s=1 - sec)
 
-    def input_gradient(message, cot, saved, value_of, gains, table, kept, place_in):
+    def input_gradient(message, base, saved, kept, place_in):
         message = jnp.concatenate([message, jnp.zeros((LANES - 8, T), F32)], axis=0).T
         scale = kept[:, 2:3]
         slope = message[:, 1:2] * kept[:, 0:1] * kept[:, 1:2]
         inner = message[:, 0:1] + slope * kept[:, 3:4]
         pull = scale * scale * scale * (inner / D)
-        for n in range(halves):
-            part = slice(n * half_rows, (n + 1) * half_rows)
-            lean = jnp.zeros((half_rows, F), F32)
-            for e in range(E):
-                sign = jnp.where(kept[part, 20:21] == e, 1.0, 0.0) - jnp.where(kept[part, 21:22] == e, 1.0, 0.0)
-                lean = lean + sign * table[e:e + 1, :]
-            grad = value_of[part, :].astype(F32) + slope[part] * lean * gains[...]
-            out_ref[place_in, part, :] = (
-                cot[part, :].astype(F32) + scale[part] * grad - saved[part, :].astype(F32) * pull[part]
-            ).astype(BF16)
+        out_ref[place_in] = (base() + slope * leans[place_in] - saved[...].astype(F32) * pull).astype(BF16)
 
     @pl.when(sec == 1)
     def _():
@@ -647,16 +659,16 @@
         for m in range(1, H):
             tail_copy(m).wait_recv()
             total = total + tail_recv[m - 1]
-        input_gradient(total, cot_ref, saved_ref, mixed, gain_ref, table_ref, cols, 0)
-        for n in range(len(far)):
-            far_copy(n).wait_recv()
+        input_gradient(total, lambda: mixed[...], saved_ref, cols, 0)
         for c in range(n_cols):
             far_value_copy(c).wait_recv()
         total = jnp.zeros((8, T), F32)
         for m in range(H):
             far_tail_copy(m).wait_recv()
             total = total + far_tail[m]
-        input_gradient(total, far_cot, far_saved, far_value, far_gain, far_table, far_cols, 1)
+        input_gradient(
+            total, lambda: far_cot[...].astype(F32) + far_cols[:, 2:3] * far_value[...].astype(F32),
+            far_saved, far_cols, 1)
         for m in range(1, H):
             tail_copy(m).wait_send()
         for n in range(halves):
@@ -695,7 +707,8 @@
     cap = 3 * T // router.shape[2]
     tn = 2 * LANES if ffd % (2 * LANES) == 0 else LANES
     tw = 2 * LANES if F % (2 * LANES) == 0 else LANES
-    n_cols, all_rows = F // tw, E * cap
+    tc = LANES
+    n_cols, all_rows = F // tc, E * cap
     deep, wide = max(tn, tw), max(D, 2 * ffd)
     vmem = pl.BlockSpec(memory_space=pltpu.VMEM)
     hbm = pl.BlockSpec(memory_space=pl.ANY)
@@ -708,10 +721,10 @@
         pltpu.VMEM((2, all_rows, ffd), F32),
         pltpu.VMEM((all_rows, ffd), BF16),
         pltpu.VMEM((2, all_rows, ffd), BF16),
-        pltpu.VMEM((2, H - 1, n_cols, all_rows, tw), BF16),
-        pltpu.VMEM((2, H - 1, n_cols, all_rows, tw), BF16),
-        pltpu.VMEM((2, n_cols, all_rows, tw), F32),
-        pltpu.VMEM((2, n_cols, all_rows, tw), BF16),
+        pltpu.VMEM((2, H - 1, n_cols, all_rows, tc), BF16),
+        pltpu.VMEM((2, H - 1, n_cols, all_rows, tc), BF16),
+        pltpu.VMEM((2, n_cols, all_rows, tc), F32),
+        pltpu.VMEM((2, n_cols, all_rows, tc), BF16),
         pltpu.VMEM((2, all_rows, F), BF16),
         pltpu.VMEM((32, T), F32),
         pltpu.VMEM((H - 1, 32, T), F32),
@@ -734,6 +747,7 @@
         pltpu.VMEM((E, 8, LANES), F32),
         pltpu.VMEM((E - 1, 8, LANES), F32),
         pltpu.VMEM((all_rows, LANES), F32),
+        pltpu.VMEM((2, T, F), F32),
         dma((A_SLOTS, 2)),
         dma((R_SLOTS, 2)),
         dma((3, E)),
@@ -760,7 +774,7 @@
         dma((E,)),
     ]
     result = pl.pallas_call(
-        functools.partial(kernel, (E, H, T, F, D, ffd, cap, tn, tw)),
+        functools.partial(kernel, (E, H, T, F, D, ffd, cap, tn, tw, tc)),
         out_shape=jax.ShapeDtypeStruct((2, T, F), BF16),
         in_specs=[vmem] * 7 + [hbm] * 3,
         out_specs=vmem,

time: 121 us -> 120 us (level)
  Pallas kernels: 119 us -> 117 us
    pallas_call x1, Pallas kernels: 119 us -> 117 us  [per_device(): pl.pallas_call(functools.partial(kernel, (E, H, T, F, D, ffd, cap, tn, tw...]
where the time goes in v5:
time: 120 us
  Pallas kernels  117 us (98%)
  local copies, waits for them, and re-layouts  1.85 us (2%)
    pallas_call x1, Pallas kernels, per_device(): pl.pallas_call(functools.partial(kernel, (E, H, T, F, D, ffd, cap, tn, tw...  117 us

profile of v5, /device:TPU:0, one launch (start us, length us, event | category | flops | bytes accessed | tf_op | source)
XLA Modules:
  0.0 119.5 jit_solution(1902794734818132711)
XLA Ops:
  0.6 117.0 %relay.1 = bf16[2,128,1024]{2,1,0:T(8,128)(2,1)} custom-call(bf16[128,1024]{1,0:T(8,128)(2,1)} %bitcast.18, bf16[128,1024]{1,0:T(8,128)(2,1)} %bitcast.19, bf16[128,1024]{1,0:T(8,128)(2,1)} %bitcast.20, s32[2,128]{1,0:T(2,128)} %bitcast.22, s32[2,128]{1,0:T(2,128)} %bitcast.23, f32[1,1024]{1,0:T(1,128)} %gain_ref.1, f32[4,1024]{1,0:T(4,128)} %bitcast.21, ...), custom_call_target="tpu_custom_call" | custom-call | tf_op jit(solution)/shard_map/relay/pallas_call | solution.py:776
  117.7 1.9 %fusion = (bf16[1,128,1024]{2,1,0:T(8,128)(2,1)}, bf16[1,128,1024]{2,1,0:T(8,128)(2,1)}) fusion(bf16[2,128,1024]{2,1,0:T(8,128)(2,1)} %relay.1), kind=kLoop, calls=%fused_computation | loop fusion | bytes 1048576 | tf_op jit(solution)/shard_map/slice | solution.py:790

commit v6 on v5

--- a/solution.py
+++ b/solution.py
@@ -179,6 +179,126 @@
     def put(n, value):
         cols[:, n:n + 1] = value
 
+    order = list(range(E - 1, 0, -1))
+    inner = flip(lax.rem(me, 2), lax.rem(lax.div(me, 2), 2), 2)
+    arrivals = [1, 3, 2] if E == 4 else order
+
+    def by_class(build):
+        if E != 4:
+            build(0)
+            return
+        for kind in range(2):
+            pl.when(inner == kind)(functools.partial(build, kind))
+
+    def first_wave(tau):
+        for k in arrivals:
+            for part in parts:
+                dispatch_copy(tau, k, part).start()
+
+    parts, width = range(2), F // 2
+
+    def region(tau, expert, feature, part):
+        start = pl.multiple_of(feature * F + part * width, LANES)
+        return rows.at[tau, pl.ds(pl.multiple_of(expert * cap, 16), cap), pl.ds(start, width)]
+
+    def forward_copy(tau, piece, bit, k, part):
+        block = region(tau, exp_peer[k], hid_peer[piece], part)
+        return remote(
+            block, block, g_send.at[tau, piece + bit, k, part], g_recv.at[tau, piece + bit, k, part],
+            h=hid_peer[bit])
+
+    def forwards(tau, piece, k, part):
+        return [
+            functools.partial(forward_copy, tau, piece, bit, k, part)
+            for bit in reversed(bits_of(H)) if piece == 0 or bit < low_bit(piece)
+        ]
+
+    def forward(tau, k, some=parts):
+        for part in some:
+            for build in forwards(tau, 0, k, part):
+                build().start()
+
+    def got_piece(tau, piece, k, part):
+        block = region(tau, exp_peer[k], hid_peer[piece], part)
+        remote(
+            block, block, g_send.at[tau, piece, k, part], g_recv.at[tau, piece, k, part],
+            h=hid_peer[low_bit(piece)]).wait_recv()
+
+    def dispatch_copy(tau, k, part):
+        return remote(
+            slots.at[tau, k - 1, :, pl.ds(part * width, width)], region(tau, me, hi, part),
+            z_send.at[tau, k, part], z_recv.at[tau, k, part], e=exp_peer[k])
+
+    def dispatch(tau, base, tokens):
+        for k in order + [0]:
+            picked = dot(chosen(base, exp_peer[k]), tokens).astype(BF16)
+            if k == 0:
+                rows[tau, pl.ds(pl.multiple_of(me * cap, 16), cap), pl.ds(pl.multiple_of(hi * F, LANES), F)] = picked
+            else:
+                slots[tau, k - 1] = picked
+
+    def z_event(tau, n):
+        k = arrivals[n]
+        for part in parts:
+            block = region(tau, exp_peer[k], hi, part)
+            remote(block, block, z_send.at[tau, k, part], z_recv.at[tau, k, part], e=exp_peer[k]).wait_recv()
+            forward(tau, k, [part])
+        if tau == NXT and n == E - 2:
+            first_wave(SAV)
+        if tau == SAV and n >= E - 3:
+            by_class(lambda kind: first_wave(COT) if kind == E - 2 - n or E != 4 and n == E - 2 else None)
+        if tau + 1 == SAV and n == E - 2:
+            forward(SAV, 0)
+
+    relays = [p for top in reversed(bits_of(H)) if top > 1 for p in range(top, H, 2 * top)]
+
+    def relay(tau, k):
+        for piece in relays:
+            for part in parts:
+                got_piece(tau, piece, k, part)
+                for build in forwards(tau, piece, k, part):
+                    build().start()
+
+    def x_event(tau, n):
+        relay(tau, arrivals[n - 1] if n else 0)
+
+    def gather_events(tau):
+        events = [functools.partial(x_event, tau, 0)]
+        for n in range(E - 1):
+            events.insert(-1, functools.partial(z_event, tau, n))
+            events.append(functools.partial(x_event, tau, n + 1))
+        return events
+
+    def complete(tau):
+        for piece in range(1, H, 2):
+            for k in range(E):
+                for part in parts:
+                    got_piece(tau, piece, k, part)
+
+    def all_to_hid(src, dst, sent, recv):
+        copies = [remote(src, dst.at[m - 1], sent.at[m], recv.at[m], h=hid_peer[m]) for m in range(1, H)]
+        for copy in copies:
+            send(lambda copy=copy: copy)
+        return copies
+
+    dispatch(NXT, 2, (next_ref[...].astype(F32) * gain).astype(BF16))
+    pl.semaphore_wait(barrier, len(partners))
+    first_wave(NXT)
+    forward(NXT, 0)
+
+    stats = jnp.zeros((T, LANES), F32)
+    for offset, ref in ((0, saved_ref), (16, next_ref)):
+        values = ref[...].astype(F32)
+        stats = stats + jnp.where(lane == offset, jnp.sum(values * values, axis=1, keepdims=True), 0.0)
+        for e in range(E):
+            weights = table_ref[e:e + 1, :] * gain
+            stats = stats + jnp.where(lane == offset + 1 + e, jnp.sum(values * weights, axis=1, keepdims=True), 0.0)
+    stat_send[...] = stats.T[0:32]
+
+    stat_copies = all_to_hid(stat_send, stat_recv, s_send, s_recv)
+    dispatch(COT, 0, cot_ref[...])
+    forward(COT, 0)
+
     kept_ranks = []
     for n, base in enumerate((0, 2)):
         hits = jnp.where(lane_f == route_cols[base], 1.0, 0.0) + jnp.where(lane_f == route_cols[base + 1], 1.0, 0.0)
@@ -189,112 +309,8 @@
             put(16 + 2 * n + c, jnp.sum(jnp.where(lane_f == route, ranks, 0.0), axis=1, keepdims=True))
             put(20 + 2 * n + c, route)
 
-    order = list(range(E - 1, 0, -1))
-    inner = flip(lax.rem(me, 2), lax.rem(lax.div(me, 2), 2), 2)
-    arrivals = [1, 3, 2] if E == 4 else order
-
-    def by_class(build):
-        if E != 4:
-            build(0)
-            return
-        for kind in range(2):
-            pl.when(inner == kind)(functools.partial(build, kind))
-
-    def first_wave(tau):
-        for k in arrivals:
-            dispatch_copy(tau, k).start()
-
-    def region(tau, expert, feature):
-        return rows.at[tau, pl.ds(pl.multiple_of(expert * cap, 16), cap), pl.ds(pl.multiple_of(feature * F, LANES), F)]
-
-    def forward_copy(tau, piece, bit, k):
-        part = region(tau, exp_peer[k], hid_peer[piece])
-        return remote(part, part, g_send.at[tau, piece + bit, k], g_recv.at[tau, piece + bit, k], h=hid_peer[bit])
-
-    def forwards(tau, piece, k):
-        return [
-            functools.partial(forward_copy, tau, piece, bit, k)
-            for bit in reversed(bits_of(H)) if piece == 0 or bit < low_bit(piece)
-        ]
-
-    def forward(tau, k):
-        for build in forwards(tau, 0, k):
-            build().start()
-
-    def got_piece(tau, piece, k):
-        part = region(tau, exp_peer[k], hid_peer[piece])
-        remote(part, part, g_send.at[tau, piece, k], g_recv.at[tau, piece, k], h=hid_peer[low_bit(piece)]).wait_recv()
-
-    def dispatch_copy(tau, k):
-        return remote(
-            slots.at[tau, k - 1], region(tau, me, hi), z_send.at[tau, k], z_recv.at[tau, k], e=exp_peer[k])
-
-    def dispatch(tau, base, tokens):
-        for k in order + [0]:
-            picked = dot(chosen(base, exp_peer[k]), tokens).astype(BF16)
-            if k == 0:
-                rows[tau, pl.ds(pl.multiple_of(me * cap, 16), cap), pl.ds(pl.multiple_of(hi * F, LANES), F)] = picked
-            else:
-                slots[tau, k - 1] = picked
-
-    def z_event(tau, n):
-        k = arrivals[n]
-        part = region(tau, exp_peer[k], hi)
-        remote(part, part, z_send.at[tau, k], z_recv.at[tau, k], e=exp_peer[k]).wait_recv()
-        forward(tau, k)
-        if tau == NXT and n == E - 2:
-            first_wave(SAV)
-        if tau == SAV and n >= E - 3:
-            by_class(lambda kind: first_wave(COT) if kind == E - 2 - n or E != 4 and n == E - 2 else None)
-        if tau + 1 == SAV and n == E - 2:
-            forward(SAV, 0)
-
-    relays = [p for top in reversed(bits_of(H)) if top > 1 for p in range(top, H, 2 * top)]
-
-    def relay(tau, k):
-        for piece in relays:
-            got_piece(tau, piece, k)
-            for build in forwards(tau, piece, k):
-                build().start()
-
-    def x_event(tau, n):
-        relay(tau, arrivals[n - 1] if n else 0)
-
-    def gather_events(tau):
-        events = [functools.partial(x_event, tau, 0)]
-        for n in range(E - 1):
-            events.insert(-1, functools.partial(z_event, tau, n))
-            events.append(functools.partial(x_event, tau, n + 1))
-        return events
-
-    def complete(tau):
-        for piece in range(1, H, 2):
-            for k in range(E):
-                got_piece(tau, piece, k)
-
-    stats = jnp.zeros((T, LANES), F32)
-    for offset, ref in ((0, saved_ref), (16, next_ref)):
-        values = ref[...].astype(F32)
-        stats = stats + jnp.where(lane == offset, jnp.sum(values * values, axis=1, keepdims=True), 0.0)
-        for e in range(E):
-            weights = table_ref[e:e + 1, :] * gain
-            stats = stats + jnp.where(lane == offset + 1 + e, jnp.sum(values * weights, axis=1, keepdims=True), 0.0)
-    stat_send[...] = stats.T[0:32]
-
-    def all_to_hid(src, dst, sent, recv):
-        copies = [remote(src, dst.at[m - 1], sent.at[m], recv.at[m], h=hid_peer[m]) for m in range(1, H)]
-        for copy in copies:
-            send(lambda copy=copy: copy)
-        return copies
-
-    dispatch(NXT, 2, (next_ref[...].astype(F32) * gain).astype(BF16))
-    dispatch(COT, 0, cot_ref[...])
-
-    pl.semaphore_wait(barrier, len(partners))
-    stat_copies = all_to_hid(stat_send, stat_recv, s_send, s_recv)
-    first_wave(NXT)
-    forward(NXT, 0)
-    forward(COT, 0)
+    next_events, cot_events = gather_events(NXT), gather_events(COT)
+    next_events[0]()
     total = stats.T[0:32]
     for m, copy in enumerate(stat_copies):
         copy.wait_recv()
@@ -452,17 +468,8 @@
         for at, event in events:
             pl.when(index == at)(event)
 
-    next_events, cot_events = gather_events(NXT), gather_events(COT)
-    for event in next_events[:-2]:
+    for event in next_events[1:-2]:
         event()
-    lean_of(0, cols, table_ref, gain_ref)
-
-    @pl.when(sec == 0)
-    def _():
-        for n in range(len(far)):
-            far_copy(n).wait_recv()
-        lean_of(1, far_cols, far_table, far_gain)
-
     for event in next_events[-2:]:
         event()
     complete(NXT)
@@ -487,9 +494,9 @@
     tuned = E == 4 and H == 4 and n_cols == 8 and n_wide == 4 and n_tiles == 7
     saved_events = gather_events(SAV)
     if tuned:
-        up_events = at(saved_events[:6], [0, 1, 2, 3, 4, 5])
-        out_events = at(saved_events[6:], [1]) + at(cot_events[:1], [2]) + at(cot_events[2:3], [6])
-        gate_events = at(cot_events[3:5], [1, 1]) + at(wave(0, 8), [1] * 8) + at(cot_events[5:], [4, 6])
+        up_events = at(saved_events[:6], [1, 2, 3, 4, 5, 6])
+        out_events = at(saved_events[6:], [3]) + at(cot_events[:1], [4])
+        gate_events = at(cot_events[2:3], [0]) + at(cot_events[3:5], [2, 2]) + at(wave(0, 8), [2] * 8) + at(cot_events[5:], [4, 6])
         gh_events = at(downs[:4], [1, 1, 4, 5])
         back_events = at(downs[4:], [1, 1, 4, 5])
         back_spots = [6, 8, 12, 12, 14]
@@ -605,6 +612,14 @@
     dots_event()
     for c in later[1:]:
         home_event(1, c)
+    lean_of(0, cols, table_ref, gain_ref)
+
+    @pl.when(sec == 0)
+    def _():
+        for n in range(len(far)):
+            far_copy(n).wait_recv()
+        lean_of(1, far_cols, far_table, far_gain)
+
     picks = selectors(0)
     inner = jnp.zeros((T, 1), F32)
     for c in range(n_cols):
@@ -678,11 +693,12 @@
         build().wait_send()
     for tau in range(3):
         for k in range(E):
-            if k:
-                dispatch_copy(tau, k).wait_send()
-            for piece in [0] + relays:
-                for build in forwards(tau, piece, k):
-                    build().wait_send()
+            for part in parts:
+                if k:
+                    dispatch_copy(tau, k, part).wait_send()
+                for piece in [0] + relays:
+                    for build in forwards(tau, piece, k, part):
+                        build().wait_send()
     for which in range(2):
         for m in range(1, H):
             for c in range(n_cols):
@@ -750,10 +766,10 @@
         pltpu.VMEM((2, T, F), F32),
         dma((A_SLOTS, 2)),
         dma((R_SLOTS, 2)),
-        dma((3, E)),
-        dma((3, E)),
-        dma((3, H, E)),
-        dma((3, H, E)),
+        dma((3, E, 2)),
+        dma((3, E, 2)),
+        dma((3, H, E, 2)),
+        dma((3, H, E, 2)),
         dma((H,)),
         dma((H,)),
         dma((2, H, n_cols)),

time: 120 us -> 120 us (level)
  no operation moved by 1% of the time
where the time goes in v6:
time: 120 us; the launch traced here: 119 us
  Pallas kernels  117 us (98%)
  local copies, waits for them, and re-layouts  1.85 us (2%)
    pallas_call x1, Pallas kernels, per_device(): pl.pallas_call(functools.partial(kernel, (E, H, T, F, D, ffd, cap, tn, tw...  117 us

profile of v6, /device:TPU:0, one launch (start us, length us, event | category | flops | bytes accessed | tf_op | source)
XLA Modules:
  0.0 119.4 jit_solution(16280713995813029369)
XLA Ops:
  0.6 116.9 %relay.1 = bf16[2,128,1024]{2,1,0:T(8,128)(2,1)} custom-call(bf16[128,1024]{1,0:T(8,128)(2,1)} %bitcast.18, bf16[128,1024]{1,0:T(8,128)(2,1)} %bitcast.19, bf16[128,1024]{1,0:T(8,128)(2,1)} %bitcast.20, s32[2,128]{1,0:T(2,128)} %bitcast.22, s32[2,128]{1,0:T(2,128)} %bitcast.23, f32[1,1024]{1,0:T(1,128)} %gain_ref.1, f32[4,1024]{1,0:T(4,128)} %bitcast.21, ...), custom_call_target="tpu_custom_call" | custom-call | tf_op jit(solution)/shard_map/relay/pallas_call | solution.py:792
  117.6 1.9 %fusion = (bf16[1,128,1024]{2,1,0:T(8,128)(2,1)}, bf16[1,128,1024]{2,1,0:T(8,128)(2,1)}) fusion(bf16[2,128,1024]{2,1,0:T(8,128)(2,1)} %relay.1), kind=kLoop, calls=%fused_computation | loop fusion | bytes 1048576 | tf_op jit(solution)/shard_map/slice | solution.py:806
